TPU v7x, 128 devices: a whole 4x4x4 slice. The times are simulated.
128 devices in a mesh: row: 8 (over z, y_hi), col: 16 (over x, y_lo, core).
Axes of the slice: x: 4, y: 4 (y_hi: 2, y_lo: 2; y = y_hi * 2 + y_lo), z: 4, core: 2. Of those that a mesh axis runs over, the one named last changes fastest.
Arguments:
- tokens: bfloat16 [1024, 8192], P('row', 'col'), may hold values from -6 to 6
- weight_in: bfloat16 [8192, 32768], P('col', 'row'), may hold values from -0.0625 to 0.0625
- weight_out: bfloat16 [32768, 8192], P('row', 'col'), may hold values from -0.03125 to 0.03125
- upstream: bfloat16 [1024, 8192], P('row', 'col'), may hold values from -1.5 to 1.5
Outputs:
- output: bfloat16 [1024, 8192], P('row', 'col')
- grad_tokens: bfloat16 [1024, 8192], P('row', 'col')
- grad_weight_in: bfloat16 [8192, 32768], P('col', 'row')
- grad_weight_out: bfloat16 [32768, 8192], P('row', 'col')
All inputs are finite; a program needn't handle non-finite values.
Results may differ from a plain program's by a relative error of at most 0.0049.
Values may be sent and summed in bfloat16 or wider, within the bound.
No kernel may reach another device: no remote copies, remote signals or barrier semaphores. Data moves between devices by JAX's collectives and lax.ppermute only.
A program may use at most 128 MiB of HBM per device.

v0:
```python
import math

import jax
import jax.numpy as jnp
from jax import lax
from jax.experimental import pallas as pl
from jax.experimental.pallas import tpu as pltpu
from jax.sharding import PartitionSpec as P


Z, YH, X, YL, C = 4, 2, 4, 2, 2


def permutation(move):
    pairs = []
    for z in range(Z):
        for yh in range(YH):
            for x in range(X):
                for yl in range(YL):
                    for c in range(C):
                        tz, tyh, tx, tyl, tc = move(z, yh, x, yl, c)
                        source = (z * YH + yh) * (X * YL * C) + (x * YL + yl) * C + c
                        target = (tz * YH + tyh) * (X * YL * C) + (tx * YL + tyl) * C + tc
                        pairs.append((source, target))
    return pairs


SWAP_CORE = permutation(lambda z, yh, x, yl, c: (z, yh, x, yl, 1 - c))
SWAP_LO = permutation(lambda z, yh, x, yl, c: (z, yh, x, 1 - yl, c))
X_UP, _, X_DOWN = (
    permutation(lambda z, yh, x, yl, c: (z, yh, (x + k) % X, yl, c)) for k in (1, 2, 3)
)


SWAP_HI = permutation(lambda z, yh, x, yl, c: (z, 1 - yh, x, yl, c))


def row_move(k):
    return permutation(lambda z, yh, x, yl, c: ((z + k) % Z, yh, x, yl, c))


def send(value, pairs):
    return lax.ppermute(value, ("row", "col"), pairs)


def after(value, *earlier):
    return lax.optimization_barrier((value, *earlier))[0]


def gelu_value(value):
    return 0.5 * value * (1.0 + jax.scipy.special.erf(value / math.sqrt(2.0)))


def gelu_slope(value):
    normal_part = jnp.exp(-0.5 * value * value) / math.sqrt(2.0 * math.pi)
    return 0.5 * (1.0 + jax.scipy.special.erf(value / math.sqrt(2.0))) + value * normal_part


def dot(left, right, contract, tiles, dtype=jnp.float32):
    left_at, right_at = contract
    deep, tall, wide = left.shape[left_at], left.shape[1 - left_at], right.shape[1 - right_at]
    rows, columns, strip = tiles

    def kernel(left_ref, right_ref, out_ref):
        @pl.loop(0, rows // strip)
        def _(index):
            span = pl.ds(pl.multiple_of(index * strip, strip), strip)
            part = left_ref[span, :] if left_at else left_ref[:, span]
            out_ref[span, :] = lax.dot_general(
                part,
                right_ref[...],
                (((left_at,), (right_at,)), ((), ())),
                preferred_element_type=jnp.float32,
            ).astype(dtype)

    left_spec = (
        pl.BlockSpec((rows, deep), lambda i, j: (i, 0))
        if left_at
        else pl.BlockSpec((deep, rows), lambda i, j: (0, i))
    )
    right_spec = (
        pl.BlockSpec((columns, deep), lambda i, j: (j, 0))
        if right_at
        else pl.BlockSpec((deep, columns), lambda i, j: (0, j))
    )
    item = jnp.dtype(dtype).itemsize
    return pl.pallas_call(
        kernel,
        grid=(tall // rows, wide // columns),
        in_specs=[left_spec, right_spec],
        out_specs=pl.BlockSpec((rows, columns), lambda i, j: (i, j)),
        out_shape=jax.ShapeDtypeStruct((tall, wide), dtype),
        compiler_params=pltpu.CompilerParams(vmem_limit_bytes=32 << 20),
        cost_estimate=pl.CostEstimate(
            flops=2 * deep * tall * wide,
            transcendentals=0,
            bytes_accessed=2 * deep * (tall + wide) + item * tall * wide,
        ),
    )(left, right)


def narrow(value):
    return value.astype(jnp.bfloat16)


def ordered(flag, own, other, axis):
    first = jnp.where(flag == 0, own, other)
    second = jnp.where(flag == 0, other, own)
    return jnp.concatenate([first, second], axis=axis)


def halves(value, axis):
    size = value.shape[axis] // 2
    return (
        lax.slice_in_dim(value, 0, size, axis=axis),
        lax.slice_in_dim(value, size, 2 * size, axis=axis),
    )


def mine_and_other(flag, value, axis):
    low, high = halves(value, axis)
    return jnp.where(flag == 0, low, high), jnp.where(flag == 0, high, low)


def cut(value, first, last):
    return lax.slice_in_dim(value, first, last, axis=0)


def start_far(far):
    low, high = halves(narrow(far), 0)
    return (send(low, X_UP), send(high, X_DOWN)), low


def start_near(up, down, far):
    rows = far[0].shape[0]
    up = narrow(up + jnp.pad(far[0], ((0, rows), (0, 0))))
    down = narrow(down + jnp.pad(far[1], ((rows, 0), (0, 0))))
    return send(up, X_UP), send(down, X_DOWN), up, down


def finish_columns(own, near):
    total = own + near[0] + near[1]
    return total + send(narrow(total), SWAP_LO)


def gather_far(up, down):
    low, high = halves(down, 0)[0], halves(up, 0)[1]
    return send(low, X_UP), send(high, X_DOWN)


ORDER = (2, 1, 3, 0)


def compute(tokens, weight_in, weight_out, upstream):
    row, col = lax.axis_index("row"), lax.axis_index("col")
    z, x, c = row // YH, col // (YL * C), col % C
    block = 2 * tokens.shape[0]

    def ring(own):
        return [own] + [send(own, row_move(-k)) for k in (1, 2, 3)]

    def turn(blocks):
        stacked = jnp.concatenate(blocks, axis=0)
        return jnp.concatenate(
            [
                lax.dynamic_slice_in_dim(stacked, (x + j - z) % 4 * block, block, axis=0)
                for j in ORDER
            ],
            axis=0,
        )

    def split_rows(far, far_received, near, near_received):
        total = jnp.concatenate([far + far_received, near + near_received], axis=0)
        chunks = []
        for k in range(4):
            place = (z + k - x) % 4
            place = jnp.where(place == 2, 0, jnp.where(place == 0, 3, (place + 1) // 2))
            chunks.append(lax.dynamic_slice_in_dim(total, place * block, block, axis=0))
        return chunks[0], [narrow(v) for v in chunks[1:]]

    def finish_rows(own, parts):
        parts = [send(v, row_move(k)) for k, v in zip((1, 2, 3), parts)]
        mine, other = halves(own + parts[0] + parts[1] + parts[2], 0)
        return mine, send(other, SWAP_HI), other

    tokens = jnp.concatenate([tokens, send(tokens, SWAP_HI)], axis=0)
    upstream = jnp.concatenate([upstream, send(upstream, SWAP_HI)], axis=0)
    tokens_ring = ring(tokens)
    in_mine, in_other = mine_and_other(c, weight_in, 1)
    in_received = send(in_other, SWAP_CORE)
    out_mine, out_other = mine_and_other(c, weight_out, 0)
    upstream_ring = ring(upstream)
    turned = turn(tokens_ring)
    all_tokens = jnp.concatenate([turned, send(turned, SWAP_CORE)], axis=1)
    w_in = jnp.concatenate([in_mine, in_received], axis=0)
    out_received = send(out_other, SWAP_CORE)
    w_out = jnp.concatenate([out_mine, out_received], axis=1)

    h_far, sent = start_far(dot(cut(all_tokens, 0, block), w_in, (1, 0), (256, 512, 256)))
    h_part = dot(after(cut(all_tokens, block, 4 * block), sent), w_in, (1, 0), (768, 512, 256))
    h_near = start_near(cut(h_part, 0, block), cut(h_part, block, 2 * block), h_far)
    upstream_ring = lax.optimization_barrier((*upstream_ring, *h_near[2:]))[:4]
    turned = turn(upstream_ring)
    all_upstream = jnp.concatenate([turned, send(turned, SWAP_CORE)], axis=1)
    g_part = dot(all_upstream, w_out, (1, 1), (1024, 512, 256))
    g_far, sent = start_far(cut(g_part, 0, block))
    hidden = finish_columns(after(cut(h_part, 2 * block, 3 * block), sent), h_near)
    g_near = start_near(cut(g_part, block, 2 * block), cut(g_part, 2 * block, 3 * block), g_far)

    act, slope = lax.optimization_barrier((narrow(gelu_value(hidden)), gelu_slope(hidden)))
    a_up, a_down = send(act, X_DOWN), send(act, X_UP)
    grad_act = finish_columns(after(cut(g_part, 3 * block, 4 * block), act), g_near)
    a_low, a_high = gather_far(a_up, a_down)
    grad_hidden = narrow(grad_act * slope)
    b_up, b_down = send(grad_hidden, X_DOWN), send(grad_hidden, X_UP)

    act_near = jnp.concatenate([after(a_up, grad_hidden), a_down, act], axis=0)
    mine, other = halves(dot(act_near, w_out, (1, 0), (768, 512, 256)), 1)
    near = mine, send(other, SWAP_CORE)
    act_far = jnp.concatenate([after(a_low, other), a_high], axis=0)
    mine, other = halves(dot(act_far, w_out, (1, 0), (256, 512, 256)), 1)
    far = mine, send(other, SWAP_CORE)
    all_act = jnp.concatenate([after(act_far, other), act_near], axis=0)
    part = dot(all_act, all_upstream, (0, 0), (512, 1024, 256), jnp.bfloat16)
    out_part, other = halves(part, 1)
    out_received = send(other, SWAP_CORE)
    own, parts = split_rows(after(far[0], other), far[1], *near)
    o_mine, o_received, _ = finish_rows(own, parts)
    b_low, b_high = gather_far(after(b_up, *parts), b_down)

    grad_near = jnp.concatenate([b_up, b_down, grad_hidden], axis=0)
    mine, other = halves(dot(grad_near, w_in, (1, 1), (768, 512, 256)), 1)
    near = mine, send(other, SWAP_CORE)
    grad_far = jnp.concatenate([after(b_low, other), b_high], axis=0)
    mine, other = halves(dot(grad_far, w_in, (1, 1), (256, 512, 256)), 1)
    far = mine, send(other, SWAP_CORE)
    own, parts = split_rows(*far, *near)
    all_grad = jnp.concatenate([after(grad_far, own, *parts), grad_near], axis=0)
    part = dot(all_tokens, all_grad, (0, 0), (512, 1024, 256), jnp.bfloat16)
    in_part, other = halves(part, 0)
    in_received = send(other, SWAP_CORE)
    out_received = after(out_received, part)
    grad_weight_out = ordered(c, out_part, out_received, 0)
    r_mine, r_received, r_other = finish_rows(after(own, part), parts)

    output = narrow(o_mine + o_received)
    in_received = after(in_received, r_other)
    grad_weight_in = ordered(c, in_part, in_received, 1)
    grad_tokens = narrow(r_mine + r_received)
    return (output, grad_tokens, grad_weight_in, grad_weight_out)


def solution(mesh):
    return jax.shard_map(
        compute,
        mesh=mesh,
        in_specs=(P("row", "col"), P("col", "row"), P("row", "col"), P("row", "col")),
        out_specs=(P("row", "col"), P("row", "col"), P("col", "row"), P("row", "col")),
        check_vma=False,
    )
```

profile of v0, /device:TPU:0, one launch (start us, length us, event | category | flops | bytes accessed | tf_op | source)
XLA Modules:
  0.0 273.4 jit_solution(16089504710250889067)
XLA Ops:
  0.6 3.4 %collective-permute-start = (bf16[128,512]{1,0:T(8,128)(2,1)}, bf16[128,512]{1,0:T(8,128)(2,1)S(1)}, u32[]{:S(2)}, u32[]{:S(2)}) collective-permute-start(bf16[128,512]{1,0:T(8,128)(2,1)} %param.4), channel_id=1, source_target_pairs={{0,16},{1,17},{2,18},{3,19},{4,20},{5,21},{6,22},{7,23},{8,24},{9,... | collective-permute-start | bytes 393224 | tf_op jit(solution)/shard_map/ppermute | solution.py:43
  5.0 2.7 %collective-permute-done = bf16[128,512]{1,0:T(8,128)(2,1)S(1)} collective-permute-done((bf16[128,512]{1,0:T(8,128)(2,1)}, bf16[128,512]{1,0:T(8,128)(2,1)S(1)}, u32[]{:S(2)}, u32[]{:S(2)}) %collective-permute-start) | collective-permute-done | bytes 131104 | tf_op jit(solution)/shard_map/ppermute | solution.py:43
  7.7 4.2 %collective-permute-start.1 = (bf16[256,512]{1,0:T(8,128)(2,1)S(1)}, bf16[256,512]{1,0:T(8,128)(2,1)S(1)}, u32[]{:S(2)}, u32[]{:S(2)}) collective-permute-start(bf16[256,512]{1,0:T(8,128)(2,1)S(1)} %get-tuple-element.78), channel_id=1, source_target_pairs={{0,96},{1,97},{2,98},{3,99},{4,100},{5,101},{6,102},{7,103},{8,104... | collective-permute-start | bytes 786440 | tf_op jit(solution)/shard_map/ppermute | solution.py:43
  11.9 4.5 %broadcast_select_fusion.7 = (bf16[512,2048]{1,0:T(8,128)(2,1)}, bf16[512,2048]{1,0:T(8,128)(2,1)}) fusion(pred[]{:T(512)S(6)} %eq.60, bf16[512,4096]{1,0:T(8,128)(2,1)} %param.5), kind=kLoop, calls=%fused_computation.52 | loop fusion | flops 2097152 | bytes 8388609 | tf_op jit(solution)/shard_map/jit(_where)/select_n | solution.py:122
  16.4 1.3 collective-permute-start.3
  17.7 9.4 %collective-permute-done.2 = bf16[256,512]{1,0:T(8,128)(2,1)S(1)} collective-permute-done((bf16[256,512]{1,0:T(8,128)(2,1)S(1)}, bf16[256,512]{1,0:T(8,128)(2,1)S(1)}, u32[]{:S(2)}, u32[]{:S(2)}) %collective-permute-start.2) | collective-permute-done | bytes 262176 | tf_op jit(solution)/shard_map/ppermute | solution.py:43
  27.2 4.8 %collective-permute-done.3 = bf16[256,512]{1,0:T(8,128)(2,1)S(1)} collective-permute-done((bf16[256,512]{1,0:T(8,128)(2,1)S(1)}, bf16[256,512]{1,0:T(8,128)(2,1)S(1)}, u32[]{:S(2)}, u32[]{:S(2)}) %collective-permute-start.3) | collective-permute-done | bytes 262176 | tf_op jit(solution)/shard_map/ppermute | solution.py:43
  32.9 3.2 %collective-permute-start.6 = (bf16[128,512]{1,0:T(8,128)(2,1)S(1)}, bf16[128,512]{1,0:T(8,128)(2,1)S(1)}, u32[]{:S(2)}, u32[]{:S(2)}) collective-permute-start(bf16[128,512]{1,0:T(8,128)(2,1)S(1)} %copy-done.26), channel_id=1, source_target_pairs={{0,16},{1,17},{2,18},{3,19},{4,20},{5,21},{6,22},{7,23},{8,24},{9,... | collective-permute-start | bytes 393224 | tf_op jit(solution)/shard_map/ppermute | solution.py:43
  36.8 1.1 copy-done.16
  37.9 2.2 pad_maximum_fusion.right_ref
  40.1 2.3 shard_map.75
  42.7 2.8 %collective-permute-start.11 = (bf16[128,2048]{1,0:T(8,128)(2,1)S(1)}, bf16[128,2048]{1,0:T(8,128)(2,1)S(1)}, u32[]{:S(2)}, u32[]{:S(2)}) collective-permute-start(bf16[128,2048]{1,0:T(8,128)(2,1)S(1)} %get-tuple-element.72), channel_id=1, source_target_pairs={{0,12},{1,13},{2,14},{3,15},{4,0},{5,1},{6,2},{7,3},{8,4},{9,5},{1... | collective-permute-start | bytes 1572872 | tf_op jit(solution)/shard_map/ppermute | solution.py:43
  45.6 2.3 collective-permute-start.8
  48.1 6.0 %shard_map.76 = f32[768,2048]{1,0:T(8,128)S(1)} custom-call(bf16[768,1024]{1,0:T(8,128)(2,1)S(1)} %slice.148.left_ref, bf16[1024,2048]{1,0:T(8,128)(2,1)S(1)} %pad_maximum_fusion.right_ref), custom_call_target="tpu_custom_call" | custom-call | flops 3221225472 | bytes 12058624 | tf_op jit(solution)/shard_map/pallas_call | solution.py:87
  54.1 2.3 collective-permute-done.11
  57.3 2.5 collective-permute-done.10
  60.7 2.7 collective-permute-done.7
  64.3 1.3 collective-permute-start.14
  65.6 2.6 collective-permute-start.15
  68.5 8.2 %shard_map.77 = f32[1024,2048]{1,0:T(8,128)S(1)} custom-call(bf16[1024,1024]{1,0:T(8,128)(2,1)S(1)} %pad_maximum_fusion.9.left_ref.right_ref, bf16[2048,1024]{1,0:T(8,128)(2,1)S(1)} %pad_maximum_fusion.1.right_ref), custom_call_target="tpu_custom_call" | custom-call | flops 4294967296 | bytes 14680064 | tf_op jit(solution)/shard_map/pallas_call | solution.py:87
  76.7 1.3 copy-done.9
  78.8 3.2 %collective-permute-start.22 = (bf16[128,2048]{1,0:T(8,128)(2,1)S(1)}, bf16[128,2048]{1,0:T(8,128)(2,1)S(1)}, u32[]{:S(2)}, u32[]{:S(2)}) collective-permute-start(bf16[128,2048]{1,0:T(8,128)(2,1)S(1)} %get-tuple-element.54), channel_id=1, source_target_pairs={{0,12},{1,13},{2,14},{3,15},{4,0},{5,1},{6,2},{7,3},{8,4},{9,5},{1... | collective-permute-start | bytes 1572872 | tf_op jit(solution)/shard_map/ppermute | solution.py:43
  82.1 10.0 %collective-permute-done.14 = bf16[256,2048]{1,0:T(8,128)(2,1)S(1)} collective-permute-done((bf16[256,2048]{1,0:T(8,128)(2,1)S(1)}, bf16[256,2048]{1,0:T(8,128)(2,1)S(1)}, u32[]{:S(2)}, u32[]{:S(2)}) %collective-permute-start.14) | collective-permute-done | bytes 1048608 | tf_op jit(solution)/shard_map/ppermute | solution.py:43
  93.5 9.0 %collective-permute-done.22 = bf16[128,2048]{1,0:T(8,128)(2,1)S(1)} collective-permute-done((bf16[128,2048]{1,0:T(8,128)(2,1)S(1)}, bf16[128,2048]{1,0:T(8,128)(2,1)S(1)}, u32[]{:S(2)}, u32[]{:S(2)}) %collective-permute-start.22) | collective-permute-done | bytes 524320 | tf_op jit(solution)/shard_map/ppermute | solution.py:43
  104.0 1.2 collective-permute-start.21
  105.2 2.1 collective-permute-start.23
  107.3 10.3 %collective-permute-done.16 = bf16[256,2048]{1,0:T(8,128)(2,1)S(1)} collective-permute-done((bf16[256,2048]{1,0:T(8,128)(2,1)S(1)}, bf16[256,2048]{1,0:T(8,128)(2,1)S(1)}, u32[]{:S(2)}, u32[]{:S(2)}) %collective-permute-start.16) | collective-permute-done | bytes 1048608 | tf_op jit(solution)/shard_map/ppermute | solution.py:43
  117.6 2.3 fusion.3
  120.0 2.7 %collective-permute-start.19 = (bf16[256,2048]{1,0:T(8,128)(2,1)S(1)}, bf16[256,2048]{1,0:T(8,128)(2,1)}, u32[]{:S(2)}, u32[]{:S(2)}) collective-permute-start(bf16[256,2048]{1,0:T(8,128)(2,1)S(1)} %get-tuple-element.29), channel_id=1, source_target_pairs={{0,12},{1,13},{2,14},{3,15},{4,0},{5,1},{6,2},{7,3},{8,4},{9,5},{1... | collective-permute-start | bytes 3145736 | tf_op jit(solution)/shard_map/ppermute | solution.py:43
  122.7 8.6 %collective-permute-done.21 = bf16[256,2048]{1,0:T(8,128)(2,1)S(1)} collective-permute-done((bf16[256,2048]{1,0:T(8,128)(2,1)S(1)}, bf16[256,2048]{1,0:T(8,128)(2,1)S(1)}, u32[]{:S(2)}, u32[]{:S(2)}) %collective-permute-start.21) | collective-permute-done | bytes 1048608 | tf_op jit(solution)/shard_map/ppermute | solution.py:43
  131.3 1.7 fusion.9
  133.8 18.4 %collective-permute-done.19 = bf16[256,2048]{1,0:T(8,128)(2,1)} collective-permute-done((bf16[256,2048]{1,0:T(8,128)(2,1)S(1)}, bf16[256,2048]{1,0:T(8,128)(2,1)}, u32[]{:S(2)}, u32[]{:S(2)}) %collective-permute-start.19) | collective-permute-done | bytes 1048608 | tf_op jit(solution)/shard_map/ppermute | solution.py:43
  153.3 3.7 %collective-permute-start.25 = (bf16[128,2048]{1,0:T(8,128)(2,1)S(1)}, bf16[128,2048]{1,0:T(8,128)(2,1)S(1)}, u32[]{:S(2)}, u32[]{:S(2)}) collective-permute-start(bf16[128,2048]{1,0:T(8,128)(2,1)S(1)} %slice.162), channel_id=1, source_target_pairs={{0,12},{1,13},{2,14},{3,15},{4,0},{5,1},{6,2},{7,3},{8,4},{9,5},{1... | collective-permute-start | bytes 1572872 | tf_op jit(solution)/shard_map/ppermute | solution.py:43
  156.9 1.1 slice.156
  158.2 3.3 %multiply_convert_fusion = bf16[256,2048]{1,0:T(8,128)(2,1)S(1)} fusion(f32[256,2048]{1,0:T(8,128)} %get-tuple-element.31, bf16[256,2048]{1,0:T(8,128)(2,1)} %collective-permute-done.24, bf16[256,2048]{1,0:T(8,128)(2,1)S(1)} %copy-done.25, f32[256,2048]{1,0:T(8,128)} %copy-done.11, bf16[256,2048]{1,0:T(8,128)(2,1)S(1)} %copy-done.23), kind=kLoop, calls=%fused_computation.39 | loop fusion | flops 4194304 | bytes 8388608 | tf_op jit(solution)/shard_map/convert_element_type | solution.py:103
  161.5 3.3 %collective-permute-start.34 = (bf16[256,2048]{1,0:T(8,128)(2,1)S(1)}, bf16[256,2048]{1,0:T(8,128)(2,1)S(1)}, u32[]{:S(2)}, u32[]{:S(2)}) collective-permute-start(bf16[256,2048]{1,0:T(8,128)(2,1)S(1)} %multiply_convert_fusion), channel_id=1, source_target_pairs={{0,12},{1,13},{2,14},{3,15},{4,0},{5,1},{6,2},{7,3},{8,4},{9,5},{1... | collective-permute-start | bytes 3145736 | tf_op jit(solution)/shard_map/ppermute | solution.py:43
  164.8 1.7 pad_maximum_fusion.6.left_ref
  166.5 4.8 %shard_map.78 = f32[768,1024]{1,0:T(8,128)S(1)} custom-call(bf16[768,2048]{1,0:T(8,128)(2,1)S(1)} %pad_maximum_fusion.6.left_ref, bf16[2048,1024]{1,0:T(8,128)(2,1)S(1)} %copy-done.4), custom_call_target="tpu_custom_call" | custom-call | flops 3221225472 | bytes 10485760 | tf_op jit(solution)/shard_map/pallas_call | solution.py:87
  171.5 2.6 collective-permute-done.18
  174.2 1.8 shard_map.79
  176.2 1.9 pad_maximum_fusion.2.left_ref
  178.3 6.3 %shard_map.80 = bf16[2048,1024]{1,0:T(8,128)(2,1)S(1)} custom-call(bf16[1024,2048]{1,0:T(8,128)(2,1)S(1)} %pad_maximum_fusion.2.left_ref, bf16[1024,1024]{1,0:T(8,128)(2,1)S(1)} %copy-done.10), custom_call_target="tpu_custom_call" | custom-call | flops 4294967296 | bytes 10485760 | tf_op jit(solution)/shard_map/pallas_call | solution.py:87
  184.7 1.7 slice.165
  187.4 6.7 %collective-permute-done.32 = bf16[256,2048]{1,0:T(8,128)(2,1)S(1)} collective-permute-done((bf16[256,2048]{1,0:T(8,128)(2,1)S(1)}, bf16[256,2048]{1,0:T(8,128)(2,1)S(1)}, u32[]{:S(2)}, u32[]{:S(2)}) %collective-permute-start.32) | collective-permute-done | bytes 1048608 | tf_op jit(solution)/shard_map/ppermute | solution.py:43
  195.6 2.0 copy-done.1
  197.6 4.7 %shard_map.81 = f32[768,1024]{1,0:T(8,128)S(1)} custom-call(bf16[768,2048]{1,0:T(8,128)(2,1)S(1)} %pad_maximum_fusion.7.left_ref, bf16[1024,2048]{1,0:T(8,128)(2,1)S(1)} %copy-done.1), custom_call_target="tpu_custom_call" | custom-call | flops 3221225472 | bytes 10485760 | tf_op jit(solution)/shard_map/pallas_call | solution.py:87
  202.3 1.5 slice.170
  204.5 1.5 fusion.24
  206.9 1.2 collective-permute-start.35
  208.2 3.6 %collective-permute-start.29 = (bf16[256,512]{1,0:T(8,128)(2,1)}, bf16[256,512]{1,0:T(8,128)(2,1)S(1)}, u32[]{:S(2)}, u32[]{:S(2)}) collective-permute-start(bf16[256,512]{1,0:T(8,128)(2,1)} %get-tuple-element.64), channel_id=1, source_target_pairs={{0,64},{1,65},{2,66},{3,67},{4,68},{5,69},{6,70},{7,71},{8,72},{9,... | collective-permute-start | bytes 786440 | tf_op jit(solution)/shard_map/ppermute | solution.py:43
  211.8 9.5 %collective-permute-done.35 = bf16[128,2048]{1,0:T(8,128)(2,1)} collective-permute-done((bf16[128,2048]{1,0:T(8,128)(2,1)}, bf16[128,2048]{1,0:T(8,128)(2,1)}, u32[]{:S(2)}, u32[]{:S(2)}) %collective-permute-start.35) | collective-permute-done | bytes 524320 | tf_op jit(solution)/shard_map/ppermute | solution.py:43
  221.3 2.1 collective-permute-start.30
  224.5 2.2 copy-done.2
  226.7 1.6 shard_map.82
  229.1 1.7 collective-permute-start.31
  230.8 1.8 slice_add_fusion.4
  235.2 7.1 %shard_map.83 = bf16[1024,2048]{1,0:T(8,128)(2,1)S(1)} custom-call(bf16[1024,1024]{1,0:T(8,128)(2,1)S(1)} %pad_maximum_fusion.8.left_ref, bf16[1024,2048]{1,0:T(8,128)(2,1)S(1)} %pad_maximum_fusion.3.right_ref), custom_call_target="tpu_custom_call" | custom-call | flops 4294967296 | bytes 10485760 | tf_op jit(solution)/shard_map/pallas_call | solution.py:87
  243.4 4.6 %collective-permute-start.39 = (bf16[256,512]{1,0:T(8,128)(2,1)S(1)}, bf16[256,512]{1,0:T(8,128)(2,1)S(1)}, u32[]{:S(2)}, u32[]{:S(2)}) collective-permute-start(bf16[256,512]{1,0:T(8,128)(2,1)S(1)} %get-tuple-element.61), channel_id=1, source_target_pairs={{0,64},{1,65},{2,66},{3,67},{4,68},{5,69},{6,70},{7,71},{8,72},{9,... | collective-permute-start | bytes 786440 | tf_op jit(solution)/shard_map/ppermute | solution.py:43
  248.3 5.2 %collective-permute-done.38 = bf16[256,512]{1,0:T(8,128)(2,1)S(1)} collective-permute-done((bf16[256,512]{1,0:T(8,128)(2,1)S(1)}, bf16[256,512]{1,0:T(8,128)(2,1)S(1)}, u32[]{:S(2)}, u32[]{:S(2)}) %collective-permute-start.38) | collective-permute-done | bytes 262176 | tf_op jit(solution)/shard_map/ppermute | solution.py:43
  253.5 6.8 %collective-permute-done.39 = bf16[256,512]{1,0:T(8,128)(2,1)S(1)} collective-permute-done((bf16[256,512]{1,0:T(8,128)(2,1)S(1)}, bf16[256,512]{1,0:T(8,128)(2,1)S(1)}, u32[]{:S(2)}, u32[]{:S(2)}) %collective-permute-start.39) | collective-permute-done | bytes 262176 | tf_op jit(solution)/shard_map/ppermute | solution.py:43
  260.4 2.2 collective-permute-start.41
  262.6 2.3 pad_maximum_fusion.5
  264.9 5.0 %collective-permute-done.41 = f32[128,512]{1,0:T(8,128)S(1)} collective-permute-done((f32[128,512]{1,0:T(8,128)S(1)}, f32[128,512]{1,0:T(8,128)S(1)}, u32[]{:S(2)}, u32[]{:S(2)}) %collective-permute-start.41) | collective-permute-done | bytes 262176 | tf_op jit(solution)/shard_map/ppermute | solution.py:43
  270.8 2.5 pad_maximum_fusion.4
  (155 shorter events, 23.1 us)
Async XLA Ops:
  0.6 7.1 %collective-permute-start = (bf16[128,512]{1,0:T(8,128)(2,1)}, bf16[128,512]{1,0:T(8,128)(2,1)S(1)}, u32[]{:S(2)}, u32[]{:S(2)}) collective-permute-start(bf16[128,512]{1,0:T(8,128)(2,1)} %param.4), channel_id=1, source_target_pairs={{0,16},{1,17},{2,18},{3,19},{4,20},{5,21},{6,22},{7,23},{8,24},{9,... | collective-permute-start | bytes 393224 | tf_op jit(solution)/shard_map/ppermute | solution.py:43
  7.7 9.9 %collective-permute-start.1 = (bf16[256,512]{1,0:T(8,128)(2,1)S(1)}, bf16[256,512]{1,0:T(8,128)(2,1)S(1)}, u32[]{:S(2)}, u32[]{:S(2)}) collective-permute-start(bf16[256,512]{1,0:T(8,128)(2,1)S(1)} %get-tuple-element.78), channel_id=1, source_target_pairs={{0,96},{1,97},{2,98},{3,99},{4,100},{5,101},{6,102},{7,103},{8,104... | collective-permute-start | bytes 786440 | tf_op jit(solution)/shard_map/ppermute | solution.py:43
  16.4 20.4 %collective-permute-start.5 = (bf16[512,2048]{1,0:T(8,128)(2,1)}, bf16[512,2048]{1,0:T(8,128)(2,1)}, u32[]{:S(2)}, u32[]{:S(2)}) collective-permute-start(bf16[512,2048]{1,0:T(8,128)(2,1)} %get-tuple-element.59), channel_id=1, source_target_pairs={{0,1},{1,0},{2,3},{3,2},{4,5},{5,4},{6,7},{7,6},{8,9},{9,8},{10,11... | collective-permute-start | bytes 6291464 | tf_op jit(solution)/shard_map/ppermute | solution.py:43
  16.4 10.7 %collective-permute-start.2 = (bf16[256,512]{1,0:T(8,128)(2,1)S(1)}, bf16[256,512]{1,0:T(8,128)(2,1)S(1)}, u32[]{:S(2)}, u32[]{:S(2)}) collective-permute-start(bf16[256,512]{1,0:T(8,128)(2,1)S(1)} %get-tuple-element.78), channel_id=1, source_target_pairs={{0,64},{1,65},{2,66},{3,67},{4,68},{5,69},{6,70},{7,71},{8,72},{9,... | collective-permute-start | bytes 786440 | tf_op jit(solution)/shard_map/ppermute | solution.py:43
  16.4 15.5 %collective-permute-start.3 = (bf16[256,512]{1,0:T(8,128)(2,1)S(1)}, bf16[256,512]{1,0:T(8,128)(2,1)S(1)}, u32[]{:S(2)}, u32[]{:S(2)}) collective-permute-start(bf16[256,512]{1,0:T(8,128)(2,1)S(1)} %get-tuple-element.78), channel_id=1, source_target_pairs={{0,32},{1,33},{2,34},{3,35},{4,36},{5,37},{6,38},{7,39},{8,40},{9,... | collective-permute-start | bytes 786440 | tf_op jit(solution)/shard_map/ppermute | solution.py:43
  32.0 4.1 %copy-start.21 = (bf16[4096,512]{1,0:T(8,128)(2,1)S(1)}, bf16[4096,512]{1,0:T(8,128)(2,1)}, u32[]{:S(2)}) copy-start(bf16[4096,512]{1,0:T(8,128)(2,1)} %param.6) | copy-start | bytes 12582916
  32.2 4.3 %collective-permute-start.4 = (bf16[1024,512]{1,0:T(8,128)(2,1)S(1)}, bf16[1024,512]{1,0:T(8,128)(2,1)S(1)}, u32[]{:S(2)}, u32[]{:S(2)}) collective-permute-start(bf16[1024,512]{1,0:T(8,128)(2,1)S(1)} %pad_maximum_fusion.10), channel_id=1, source_target_pairs={{0,1},{1,0},{2,3},{3,2},{4,5},{5,4},{6,7},{7,6},{8,9},{9,8},{10,11... | collective-permute-start | bytes 3145736 | tf_op jit(solution)/shard_map/ppermute | solution.py:43
  32.9 12.6 %collective-permute-start.6 = (bf16[128,512]{1,0:T(8,128)(2,1)S(1)}, bf16[128,512]{1,0:T(8,128)(2,1)S(1)}, u32[]{:S(2)}, u32[]{:S(2)}) collective-permute-start(bf16[128,512]{1,0:T(8,128)(2,1)S(1)} %copy-done.26), channel_id=1, source_target_pairs={{0,16},{1,17},{2,18},{3,19},{4,20},{5,21},{6,22},{7,23},{8,24},{9,... | collective-permute-start | bytes 393224 | tf_op jit(solution)/shard_map/ppermute | solution.py:43
  36.4 27.4 %collective-permute-start.13 = (bf16[2048,512]{1,0:T(8,128)(2,1)S(1)}, bf16[2048,512]{1,0:T(8,128)(2,1)S(1)}, u32[]{:S(2)}, u32[]{:S(2)}) collective-permute-start(bf16[2048,512]{1,0:T(8,128)(2,1)S(1)} %get-tuple-element.57), channel_id=1, source_target_pairs={{0,1},{1,0},{2,3},{3,2},{4,5},{5,4},{6,7},{7,6},{8,9},{9,8},{10,11... | collective-permute-start | bytes 6291464 | tf_op jit(solution)/shard_map/ppermute | solution.py:43
  40.1 8.0 %copy-start = (bf16[1024,2048]{1,0:T(8,128)(2,1)}, bf16[1024,2048]{1,0:T(8,128)(2,1)S(1)}, u32[]{:S(2)}) copy-start(bf16[1024,2048]{1,0:T(8,128)(2,1)S(1)} %pad_maximum_fusion.right_ref) | copy-start | bytes 12582916
  42.7 13.8 %collective-permute-start.11 = (bf16[128,2048]{1,0:T(8,128)(2,1)S(1)}, bf16[128,2048]{1,0:T(8,128)(2,1)S(1)}, u32[]{:S(2)}, u32[]{:S(2)}) collective-permute-start(bf16[128,2048]{1,0:T(8,128)(2,1)S(1)} %get-tuple-element.72), channel_id=1, source_target_pairs={{0,12},{1,13},{2,14},{3,15},{4,0},{5,1},{6,2},{7,3},{8,4},{9,5},{1... | collective-permute-start | bytes 1572872 | tf_op jit(solution)/shard_map/ppermute | solution.py:43
  45.5 14.4 %collective-permute-start.10 = (bf16[128,2048]{1,0:T(8,128)(2,1)S(1)}, bf16[128,2048]{1,0:T(8,128)(2,1)S(1)}, u32[]{:S(2)}, u32[]{:S(2)}) collective-permute-start(bf16[128,2048]{1,0:T(8,128)(2,1)S(1)} %get-tuple-element.73), channel_id=1, source_target_pairs={{0,4},{1,5},{2,6},{3,7},{4,8},{5,9},{6,10},{7,11},{8,12},{9,13},{1... | collective-permute-start | bytes 1572872 | tf_op jit(solution)/shard_map/ppermute | solution.py:43
  45.5 15.2 %collective-permute-start.9 = (bf16[256,512]{1,0:T(8,128)(2,1)S(1)}, bf16[256,512]{1,0:T(8,128)(2,1)S(1)}, u32[]{:S(2)}, u32[]{:S(2)}) collective-permute-start(bf16[256,512]{1,0:T(8,128)(2,1)S(1)} %constant_dynamic-update-slice_fusion.7), channel_id=1, source_target_pairs={{0,32},{1,33},{2,34},{3,35},{4,36},{5,37},{6,38},{7,39},{8,40},{9,... | collective-permute-start | bytes 786440 | tf_op jit(solution)/shard_map/ppermute | solution.py:43
  45.6 15.1 %collective-permute-start.8 = (bf16[256,512]{1,0:T(8,128)(2,1)S(1)}, bf16[256,512]{1,0:T(8,128)(2,1)S(1)}, u32[]{:S(2)}, u32[]{:S(2)}) collective-permute-start(bf16[256,512]{1,0:T(8,128)(2,1)S(1)} %constant_dynamic-update-slice_fusion.7), channel_id=1, source_target_pairs={{0,64},{1,65},{2,66},{3,67},{4,68},{5,69},{6,70},{7,71},{8,72},{9,... | collective-permute-start | bytes 786440 | tf_op jit(solution)/shard_map/ppermute | solution.py:43
  56.4 7.0 %collective-permute-start.7 = (bf16[256,512]{1,0:T(8,128)(2,1)S(1)}, bf16[256,512]{1,0:T(8,128)(2,1)S(1)}, u32[]{:S(2)}, u32[]{:S(2)}) collective-permute-start(bf16[256,512]{1,0:T(8,128)(2,1)S(1)} %constant_dynamic-update-slice_fusion.7), channel_id=1, source_target_pairs={{0,96},{1,97},{2,98},{3,99},{4,100},{5,101},{6,102},{7,103},{8,104... | collective-permute-start | bytes 786440 | tf_op jit(solution)/shard_map/ppermute | solution.py:43
  63.7 4.5 %collective-permute-start.12 = (bf16[1024,512]{1,0:T(8,128)(2,1)S(1)}, bf16[1024,512]{1,0:T(8,128)(2,1)S(1)}, u32[]{:S(2)}, u32[]{:S(2)}) collective-permute-start(bf16[1024,512]{1,0:T(8,128)(2,1)S(1)} %pad_maximum_fusion.11), channel_id=1, source_target_pairs={{0,1},{1,0},{2,3},{3,2},{4,5},{5,4},{6,7},{7,6},{8,9},{9,8},{10,11... | collective-permute-start | bytes 3145736 | tf_op jit(solution)/shard_map/ppermute | solution.py:43
  64.3 4.1 %copy-start.3 = (bf16[2048,1024]{1,0:T(8,128)(2,1)}, bf16[2048,1024]{1,0:T(8,128)(2,1)S(1)}, u32[]{:S(2)}) copy-start(bf16[2048,1024]{1,0:T(8,128)(2,1)S(1)} %pad_maximum_fusion.1.right_ref) | copy-start | bytes 12582916
  64.3 27.8 %collective-permute-start.14 = (bf16[256,2048]{1,0:T(8,128)(2,1)S(1)}, bf16[256,2048]{1,0:T(8,128)(2,1)S(1)}, u32[]{:S(2)}, u32[]{:S(2)}) collective-permute-start(bf16[256,2048]{1,0:T(8,128)(2,1)S(1)} %get-tuple-element.49), channel_id=1, source_target_pairs={{0,4},{1,5},{2,6},{3,7},{4,8},{5,9},{6,10},{7,11},{8,12},{9,13},{1... | collective-permute-start | bytes 3145736 | tf_op jit(solution)/shard_map/ppermute | solution.py:43
  65.6 26.5 %collective-permute-start.15 = (bf16[256,2048]{1,0:T(8,128)(2,1)S(1)}, bf16[256,2048]{1,0:T(8,128)(2,1)S(1)}, u32[]{:S(2)}, u32[]{:S(2)}) collective-permute-start(bf16[256,2048]{1,0:T(8,128)(2,1)S(1)} %get-tuple-element.50), channel_id=1, source_target_pairs={{0,12},{1,13},{2,14},{3,15},{4,0},{5,1},{6,2},{7,3},{8,4},{9,5},{1... | collective-permute-start | bytes 3145736 | tf_op jit(solution)/shard_map/ppermute | solution.py:43
  78.8 24.4 %collective-permute-start.20 = (bf16[128,2048]{1,0:T(8,128)(2,1)S(1)}, bf16[128,2048]{1,0:T(8,128)(2,1)S(1)}, u32[]{:S(2)}, u32[]{:S(2)}) collective-permute-start(bf16[128,2048]{1,0:T(8,128)(2,1)S(1)} %get-tuple-element.55), channel_id=1, source_target_pairs={{0,4},{1,5},{2,6},{3,7},{4,8},{5,9},{6,10},{7,11},{8,12},{9,13},{1... | collective-permute-start | bytes 1572872 | tf_op jit(solution)/shard_map/ppermute | solution.py:43
  78.8 23.6 %collective-permute-start.22 = (bf16[128,2048]{1,0:T(8,128)(2,1)S(1)}, bf16[128,2048]{1,0:T(8,128)(2,1)S(1)}, u32[]{:S(2)}, u32[]{:S(2)}) collective-permute-start(bf16[128,2048]{1,0:T(8,128)(2,1)S(1)} %get-tuple-element.54), channel_id=1, source_target_pairs={{0,12},{1,13},{2,14},{3,15},{4,0},{5,1},{6,2},{7,3},{8,4},{9,5},{1... | collective-permute-start | bytes 1572872 | tf_op jit(solution)/shard_map/ppermute | solution.py:43
  92.6 25.0 %collective-permute-start.16 = (bf16[256,2048]{1,0:T(8,128)(2,1)S(1)}, bf16[256,2048]{1,0:T(8,128)(2,1)S(1)}, u32[]{:S(2)}, u32[]{:S(2)}) collective-permute-start(bf16[256,2048]{1,0:T(8,128)(2,1)S(1)} %fusion.8), channel_id=1, source_target_pairs={{0,2},{1,3},{2,0},{3,1},{4,6},{5,7},{6,4},{7,5},{8,10},{9,11},{10,... | collective-permute-start | bytes 3145736 | tf_op jit(solution)/shard_map/ppermute | solution.py:43
  104.0 27.3 %copy-start.11 = (f32[256,2048]{1,0:T(8,128)}, f32[256,2048]{1,0:T(8,128)S(1)}, u32[]{:S(2)}) copy-start(f32[256,2048]{1,0:T(8,128)S(1)} %get-tuple-element.30) | copy-start | bytes 6291460
  104.0 27.3 %collective-permute-start.21 = (bf16[256,2048]{1,0:T(8,128)(2,1)S(1)}, bf16[256,2048]{1,0:T(8,128)(2,1)S(1)}, u32[]{:S(2)}, u32[]{:S(2)}) collective-permute-start(bf16[256,2048]{1,0:T(8,128)(2,1)S(1)} %get-tuple-element.42), channel_id=1, source_target_pairs={{0,4},{1,5},{2,6},{3,7},{4,8},{5,9},{6,10},{7,11},{8,12},{9,13},{1... | collective-permute-start | bytes 3145736 | tf_op jit(solution)/shard_map/ppermute | solution.py:43
  105.2 26.1 %collective-permute-start.23 = (bf16[256,2048]{1,0:T(8,128)(2,1)S(1)}, bf16[256,2048]{1,0:T(8,128)(2,1)S(1)}, u32[]{:S(2)}, u32[]{:S(2)}) collective-permute-start(bf16[256,2048]{1,0:T(8,128)(2,1)S(1)} %get-tuple-element.43), channel_id=1, source_target_pairs={{0,12},{1,13},{2,14},{3,15},{4,0},{5,1},{6,2},{7,3},{8,4},{9,5},{1... | collective-permute-start | bytes 3145736 | tf_op jit(solution)/shard_map/ppermute | solution.py:43
  120.0 32.2 %collective-permute-start.19 = (bf16[256,2048]{1,0:T(8,128)(2,1)S(1)}, bf16[256,2048]{1,0:T(8,128)(2,1)}, u32[]{:S(2)}, u32[]{:S(2)}) collective-permute-start(bf16[256,2048]{1,0:T(8,128)(2,1)S(1)} %get-tuple-element.29), channel_id=1, source_target_pairs={{0,12},{1,13},{2,14},{3,15},{4,0},{5,1},{6,2},{7,3},{8,4},{9,5},{1... | collective-permute-start | bytes 3145736 | tf_op jit(solution)/shard_map/ppermute | solution.py:43
  122.7 34.2 %collective-permute-start.17 = (bf16[256,2048]{1,0:T(8,128)(2,1)S(1)}, bf16[256,2048]{1,0:T(8,128)(2,1)}, u32[]{:S(2)}, u32[]{:S(2)}) collective-permute-start(bf16[256,2048]{1,0:T(8,128)(2,1)S(1)} %get-tuple-element.29), channel_id=1, source_target_pairs={{0,4},{1,5},{2,6},{3,7},{4,8},{5,9},{6,10},{7,11},{8,12},{9,13},{1... | collective-permute-start | bytes 3145736 | tf_op jit(solution)/shard_map/ppermute | solution.py:43
  131.3 1.8 copy-start.22
  131.3 1.8 copy-start.24
  133.1 25.0 %collective-permute-start.24 = (bf16[256,2048]{1,0:T(8,128)(2,1)}, bf16[256,2048]{1,0:T(8,128)(2,1)}, u32[]{:S(2)}, u32[]{:S(2)}) collective-permute-start(bf16[256,2048]{1,0:T(8,128)(2,1)} %fusion.9), channel_id=1, source_target_pairs={{0,2},{1,3},{2,0},{3,1},{4,6},{5,7},{6,4},{7,5},{8,10},{9,11},{10,... | collective-permute-start | bytes 3145736 | tf_op jit(solution)/shard_map/ppermute | solution.py:43
  133.8 24.4 %copy-start.23 = (bf16[256,2048]{1,0:T(8,128)(2,1)S(1)}, bf16[256,2048]{1,0:T(8,128)(2,1)}, u32[]{:S(2)}) copy-start(bf16[256,2048]{1,0:T(8,128)(2,1)} %copy-done.22) | copy-start | bytes 3145732
  133.8 24.4 %copy-start.25 = (bf16[256,2048]{1,0:T(8,128)(2,1)S(1)}, bf16[256,2048]{1,0:T(8,128)(2,1)}, u32[]{:S(2)}) copy-start(bf16[256,2048]{1,0:T(8,128)(2,1)} %copy-done.24) | copy-start | bytes 3145732
  153.3 20.9 %collective-permute-start.25 = (bf16[128,2048]{1,0:T(8,128)(2,1)S(1)}, bf16[128,2048]{1,0:T(8,128)(2,1)S(1)}, u32[]{:S(2)}, u32[]{:S(2)}) collective-permute-start(bf16[128,2048]{1,0:T(8,128)(2,1)S(1)} %slice.162), channel_id=1, source_target_pairs={{0,12},{1,13},{2,14},{3,15},{4,0},{5,1},{6,2},{7,3},{8,4},{9,5},{1... | collective-permute-start | bytes 1572872 | tf_op jit(solution)/shard_map/ppermute | solution.py:43
  158.0 16.1 %collective-permute-start.18 = (bf16[128,2048]{1,0:T(8,128)(2,1)S(1)}, bf16[128,2048]{1,0:T(8,128)(2,1)S(1)}, u32[]{:S(2)}, u32[]{:S(2)}) collective-permute-start(bf16[128,2048]{1,0:T(8,128)(2,1)S(1)} %slice.156), channel_id=1, source_target_pairs={{0,4},{1,5},{2,6},{3,7},{4,8},{5,9},{6,10},{7,11},{8,12},{9,13},{1... | collective-permute-start | bytes 1572872 | tf_op jit(solution)/shard_map/ppermute | solution.py:43
  161.5 33.6 %copy-start.14 = (bf16[256,2048]{1,0:T(8,128)(2,1)}, bf16[256,2048]{1,0:T(8,128)(2,1)S(1)}, u32[]{:S(2)}) copy-start(bf16[256,2048]{1,0:T(8,128)(2,1)S(1)} %multiply_convert_fusion) | copy-start | bytes 3145732
  161.5 5.0 %copy-start.4 = (bf16[2048,1024]{1,0:T(8,128)(2,1)S(1)}, bf16[2048,1024]{1,0:T(8,128)(2,1)}, u32[]{:S(2)}) copy-start(bf16[2048,1024]{1,0:T(8,128)(2,1)} %copy-done.3) | copy-start | bytes 12582916
  161.5 33.5 %collective-permute-start.34 = (bf16[256,2048]{1,0:T(8,128)(2,1)S(1)}, bf16[256,2048]{1,0:T(8,128)(2,1)S(1)}, u32[]{:S(2)}, u32[]{:S(2)}) collective-permute-start(bf16[256,2048]{1,0:T(8,128)(2,1)S(1)} %multiply_convert_fusion), channel_id=1, source_target_pairs={{0,12},{1,13},{2,14},{3,15},{4,0},{5,1},{6,2},{7,3},{8,4},{9,5},{1... | collective-permute-start | bytes 3145736 | tf_op jit(solution)/shard_map/ppermute | solution.py:43
  164.8 29.3 %collective-permute-start.32 = (bf16[256,2048]{1,0:T(8,128)(2,1)S(1)}, bf16[256,2048]{1,0:T(8,128)(2,1)S(1)}, u32[]{:S(2)}, u32[]{:S(2)}) collective-permute-start(bf16[256,2048]{1,0:T(8,128)(2,1)S(1)} %multiply_convert_fusion), channel_id=1, source_target_pairs={{0,4},{1,5},{2,6},{3,7},{4,8},{5,9},{6,10},{7,11},{8,12},{9,13},{1... | collective-permute-start | bytes 3145736 | tf_op jit(solution)/shard_map/ppermute | solution.py:43
  171.5 32.4 %collective-permute-start.27 = (f32[768,512]{1,0:T(8,128)S(1)}, f32[768,512]{1,0:T(8,128)S(1)}, u32[]{:S(2)}, u32[]{:S(2)}) collective-permute-start(f32[768,512]{1,0:T(8,128)S(1)} %slice.161), channel_id=1, source_target_pairs={{0,1},{1,0},{2,3},{3,2},{4,5},{5,4},{6,7},{7,6},{8,9},{9,8},{10,11... | collective-permute-start | bytes 4718600 | tf_op jit(solution)/shard_map/ppermute | solution.py:43
  176.1 2.2 copy-start.10
  176.1 11.2 %collective-permute-start.26 = (f32[256,512]{1,0:T(8,128)S(1)}, f32[256,512]{1,0:T(8,128)S(1)}, u32[]{:S(2)}, u32[]{:S(2)}) collective-permute-start(f32[256,512]{1,0:T(8,128)S(1)} %get-tuple-element.66), channel_id=1, source_target_pairs={{0,1},{1,0},{2,3},{3,2},{4,5},{5,4},{6,7},{7,6},{8,9},{9,8},{10,11... | collective-permute-start | bytes 1572872 | tf_op jit(solution)/shard_map/ppermute | solution.py:43
  184.7 2.6 copy-start.5
  195.0 2.6 copy-start.1
  195.1 13.1 %collective-permute-start.33 = (bf16[128,2048]{1,0:T(8,128)(2,1)}, bf16[128,2048]{1,0:T(8,128)(2,1)S(1)}, u32[]{:S(2)}, u32[]{:S(2)}) collective-permute-start(bf16[128,2048]{1,0:T(8,128)(2,1)} %slice.169), channel_id=1, source_target_pairs={{0,4},{1,5},{2,6},{3,7},{4,8},{5,9},{6,10},{7,11},{8,12},{9,13},{1... | collective-permute-start | bytes 1572872 | tf_op jit(solution)/shard_map/ppermute | solution.py:43
  195.1 11.0 %copy-start.17 = (bf16[256,2048]{1,0:T(8,128)(2,1)}, bf16[256,2048]{1,0:T(8,128)(2,1)S(1)}, u32[]{:S(2)}) copy-start(bf16[256,2048]{1,0:T(8,128)(2,1)S(1)} %collective-permute-done.34) | copy-start | bytes 3145732
  202.3 2.3 copy-start.7
  203.9 27.0 %collective-permute-start.37 = (f32[768,512]{1,0:T(8,128)}, f32[768,512]{1,0:T(8,128)}, u32[]{:S(2)}, u32[]{:S(2)}) collective-permute-start(f32[768,512]{1,0:T(8,128)} %slice.170), channel_id=1, source_target_pairs={{0,1},{1,0},{2,3},{3,2},{4,5},{5,4},{6,7},{7,6},{8,9},{9,8},{10,11... | collective-permute-start | bytes 4718600 | tf_op jit(solution)/shard_map/ppermute | solution.py:43
  206.9 14.4 %collective-permute-start.35 = (bf16[128,2048]{1,0:T(8,128)(2,1)}, bf16[128,2048]{1,0:T(8,128)(2,1)}, u32[]{:S(2)}, u32[]{:S(2)}) collective-permute-start(bf16[128,2048]{1,0:T(8,128)(2,1)} %slice.139), channel_id=1, source_target_pairs={{0,12},{1,13},{2,14},{3,15},{4,0},{5,1},{6,2},{7,3},{8,4},{9,5},{1... | collective-permute-start | bytes 1572872 | tf_op jit(solution)/shard_map/ppermute | solution.py:43
  208.2 39.8 %collective-permute-start.43 = (bf16[2048,512]{1,0:T(8,128)(2,1)}, bf16[2048,512]{1,0:T(8,128)(2,1)S(1)}, u32[]{:S(2)}, u32[]{:S(2)}) collective-permute-start(bf16[2048,512]{1,0:T(8,128)(2,1)} %slice.165), channel_id=1, source_target_pairs={{0,1},{1,0},{2,3},{3,2},{4,5},{5,4},{6,7},{7,6},{8,9},{9,8},{10,11... | collective-permute-start | bytes 6291464 | tf_op jit(solution)/shard_map/ppermute | solution.py:43
  208.2 20.2 %collective-permute-start.28 = (bf16[256,512]{1,0:T(8,128)(2,1)}, bf16[256,512]{1,0:T(8,128)(2,1)S(1)}, u32[]{:S(2)}, u32[]{:S(2)}) collective-permute-start(bf16[256,512]{1,0:T(8,128)(2,1)} %get-tuple-element.63), channel_id=1, source_target_pairs={{0,32},{1,33},{2,34},{3,35},{4,36},{5,37},{6,38},{7,39},{8,40},{9,... | collective-permute-start | bytes 786440 | tf_op jit(solution)/shard_map/ppermute | solution.py:43
  208.2 20.3 %collective-permute-start.29 = (bf16[256,512]{1,0:T(8,128)(2,1)}, bf16[256,512]{1,0:T(8,128)(2,1)S(1)}, u32[]{:S(2)}, u32[]{:S(2)}) collective-permute-start(bf16[256,512]{1,0:T(8,128)(2,1)} %get-tuple-element.64), channel_id=1, source_target_pairs={{0,64},{1,65},{2,66},{3,67},{4,68},{5,69},{6,70},{7,71},{8,72},{9,... | collective-permute-start | bytes 786440 | tf_op jit(solution)/shard_map/ppermute | solution.py:43
  221.3 7.6 %collective-permute-start.30 = (bf16[256,512]{1,0:T(8,128)(2,1)S(1)}, bf16[256,512]{1,0:T(8,128)(2,1)S(1)}, u32[]{:S(2)}, u32[]{:S(2)}) collective-permute-start(bf16[256,512]{1,0:T(8,128)(2,1)S(1)} %get-tuple-element.65), channel_id=1, source_target_pairs={{0,96},{1,97},{2,98},{3,99},{4,100},{5,101},{6,102},{7,103},{8,104... | collective-permute-start | bytes 786440 | tf_op jit(solution)/shard_map/ppermute | solution.py:43
  224.5 2.2 copy-start.2
  226.7 2.2 copy-start.13
  228.3 2.5 copy-start.8
  228.3 4.2 %collective-permute-start.36 = (f32[256,512]{1,0:T(8,128)S(1)}, f32[256,512]{1,0:T(8,128)S(1)}, u32[]{:S(2)}, u32[]{:S(2)}) collective-permute-start(f32[256,512]{1,0:T(8,128)S(1)} %slice.172), channel_id=1, source_target_pairs={{0,1},{1,0},{2,3},{3,2},{4,5},{5,4},{6,7},{7,6},{8,9},{9,8},{10,11... | collective-permute-start | bytes 1572872 | tf_op jit(solution)/shard_map/ppermute | solution.py:43
  229.1 13.5 %collective-permute-start.31 = (f32[128,512]{1,0:T(8,128)S(1)}, f32[128,512]{1,0:T(8,128)S(1)}, u32[]{:S(2)}, u32[]{:S(2)}) collective-permute-start(f32[128,512]{1,0:T(8,128)S(1)} %slice.168), channel_id=1, source_target_pairs={{0,16},{1,17},{2,18},{3,19},{4,20},{5,21},{6,22},{7,23},{8,24},{9,... | collective-permute-start | bytes 786440 | tf_op jit(solution)/shard_map/ppermute | solution.py:43
  232.8 1.7 copy-start.18
  242.3 5.7 %copy-start.6 = (bf16[2048,1024]{1,0:T(8,128)(2,1)S(1)}, bf16[2048,1024]{1,0:T(8,128)(2,1)}, u32[]{:S(2)}) copy-start(bf16[2048,1024]{1,0:T(8,128)(2,1)} %copy-done.5) | copy-start | bytes 12582916
  242.6 28.0 %collective-permute-start.42 = (bf16[512,2048]{1,0:T(8,128)(2,1)S(1)}, bf16[512,2048]{1,0:T(8,128)(2,1)S(1)}, u32[]{:S(2)}, u32[]{:S(2)}) collective-permute-start(bf16[512,2048]{1,0:T(8,128)(2,1)S(1)} %slice.177), channel_id=1, source_target_pairs={{0,1},{1,0},{2,3},{3,2},{4,5},{5,4},{6,7},{7,6},{8,9},{9,8},{10,11... | collective-permute-start | bytes 6291464 | tf_op jit(solution)/shard_map/ppermute | solution.py:43
  243.4 10.1 %collective-permute-start.38 = (bf16[256,512]{1,0:T(8,128)(2,1)S(1)}, bf16[256,512]{1,0:T(8,128)(2,1)S(1)}, u32[]{:S(2)}, u32[]{:S(2)}) collective-permute-start(bf16[256,512]{1,0:T(8,128)(2,1)S(1)} %get-tuple-element.60), channel_id=1, source_target_pairs={{0,32},{1,33},{2,34},{3,35},{4,36},{5,37},{6,38},{7,39},{8,40},{9,... | collective-permute-start | bytes 786440 | tf_op jit(solution)/shard_map/ppermute | solution.py:43
  243.4 16.9 %collective-permute-start.39 = (bf16[256,512]{1,0:T(8,128)(2,1)S(1)}, bf16[256,512]{1,0:T(8,128)(2,1)S(1)}, u32[]{:S(2)}, u32[]{:S(2)}) collective-permute-start(bf16[256,512]{1,0:T(8,128)(2,1)S(1)} %get-tuple-element.61), channel_id=1, source_target_pairs={{0,64},{1,65},{2,66},{3,67},{4,68},{5,69},{6,70},{7,71},{8,72},{9,... | collective-permute-start | bytes 786440 | tf_op jit(solution)/shard_map/ppermute | solution.py:43
  248.0 12.3 %collective-permute-start.40 = (bf16[256,512]{1,0:T(8,128)(2,1)S(1)}, bf16[256,512]{1,0:T(8,128)(2,1)S(1)}, u32[]{:S(2)}, u32[]{:S(2)}) collective-permute-start(bf16[256,512]{1,0:T(8,128)(2,1)S(1)} %get-tuple-element.62), channel_id=1, source_target_pairs={{0,96},{1,97},{2,98},{3,99},{4,100},{5,101},{6,102},{7,103},{8,104... | collective-permute-start | bytes 786440 | tf_op jit(solution)/shard_map/ppermute | solution.py:43
  260.4 9.4 %collective-permute-start.41 = (f32[128,512]{1,0:T(8,128)S(1)}, f32[128,512]{1,0:T(8,128)S(1)}, u32[]{:S(2)}, u32[]{:S(2)}) collective-permute-start(f32[128,512]{1,0:T(8,128)S(1)} %slice.175), channel_id=1, source_target_pairs={{0,16},{1,17},{2,18},{3,19},{4,20},{5,21},{6,22},{7,23},{8,24},{9,... | collective-permute-start | bytes 786440 | tf_op jit(solution)/shard_map/ppermute | solution.py:43
  (7 other events, 9.5 us)
where the time goes:
time: 274 us; the launch traced here: 273 us
  waiting for transfers between devices  118 us (43%)
  starting transfers between devices  55.9 us (20%)
  Pallas kernels  42.8 us (16%)
  other arithmetic  35.1 us (13%)
  local copies, waits for them, and re-layouts  20.3 us (7%)
    ppermute x44, waiting for transfers between devices, send(): return lax.ppermute(value, ('row', 'col'), pairs)  118 us
    ppermute x44, starting transfers between devices, send(): return lax.ppermute(value, ('row', 'col'), pairs)  55.9 us
    pallas_call x9, Pallas kernels, dot(): pl.pallas_call(kernel, grid=(tall // rows, wide // columns), in_specs=[le...  42.8 us
    convert_element_type x10, other arithmetic, narrow(): return value.astype(jnp.bfloat16)  11.1 us
    unnamed x63, local copies, waits for them, and re-layouts  10.8 us
    slice x12, local copies, waits for them, and re-layouts, halves(): lax.slice_in_dim(value, size, 2 * size, axis=axis)  5.96 us
  transfers between devices with their start and end apart: 44, of which 19 were waited for; matrix products, arithmetic and copies ran while one was open for 16% of the time, Pallas kernels for 16%

commit v1 on v0

--- a/solution.py
+++ b/solution.py
@@ -90,7 +90,7 @@
         in_specs=[left_spec, right_spec],
         out_specs=pl.BlockSpec((rows, columns), lambda i, j: (i, j)),
         out_shape=jax.ShapeDtypeStruct((tall, wide), dtype),
-        compiler_params=pltpu.CompilerParams(vmem_limit_bytes=32 << 20),
+        compiler_params=pltpu.CompilerParams(vmem_limit_bytes=16 << 20),
         cost_estimate=pl.CostEstimate(
             flops=2 * deep * tall * wide,
             transcendentals=0,
@@ -132,14 +132,17 @@
 
 
 def start_near(up, down, far):
-    rows = far[0].shape[0]
-    up = narrow(up + jnp.pad(far[0], ((0, rows), (0, 0))))
-    down = narrow(down + jnp.pad(far[1], ((rows, 0), (0, 0))))
-    return send(up, X_UP), send(down, X_DOWN), up, down
-
-
-def finish_columns(own, near):
-    total = own + near[0] + near[1]
+    up, down = halves(up, 0), halves(down, 0)
+    early = narrow(up[1]), narrow(down[0])
+    late = narrow(up[0] + far[0]), narrow(down[1] + far[1])
+    parts = [send(early[0], X_UP), send(early[1], X_DOWN)]
+    parts += [send(late[0], X_UP), send(late[1], X_DOWN)]
+    return parts, early, late
+
+
+def finish_columns(own, parts):
+    low, high = halves(own, 0)
+    total = jnp.concatenate([low + parts[2] + parts[1], high + parts[0] + parts[3]], axis=0)
     return total + send(narrow(total), SWAP_LO)
 
 
@@ -171,6 +174,7 @@
 
     def split_rows(far, far_received, near, near_received):
         total = jnp.concatenate([far + far_received, near + near_received], axis=0)
+        total = lax.optimization_barrier(total)
         chunks = []
         for k in range(4):
             place = (z + k - x) % 4
@@ -183,9 +187,9 @@
         mine, other = halves(own + parts[0] + parts[1] + parts[2], 0)
         return mine, send(other, SWAP_HI), other
 
-    tokens = jnp.concatenate([tokens, send(tokens, SWAP_HI)], axis=0)
+    received = send(tokens, SWAP_HI)
+    tokens_ring = [v for own, other in zip(ring(tokens), ring(received)) for v in (own, other)]
     upstream = jnp.concatenate([upstream, send(upstream, SWAP_HI)], axis=0)
-    tokens_ring = ring(tokens)
     in_mine, in_other = mine_and_other(c, weight_in, 1)
     in_received = send(in_other, SWAP_CORE)
     out_mine, out_other = mine_and_other(c, weight_out, 0)
@@ -198,18 +202,20 @@
 
     h_far, sent = start_far(dot(cut(all_tokens, 0, block), w_in, (1, 0), (256, 512, 256)))
     h_part = dot(after(cut(all_tokens, block, 4 * block), sent), w_in, (1, 0), (768, 512, 256))
-    h_near = start_near(cut(h_part, 0, block), cut(h_part, block, 2 * block), h_far)
-    upstream_ring = lax.optimization_barrier((*upstream_ring, *h_near[2:]))[:4]
+    h_parts, _, late = start_near(cut(h_part, 0, block), cut(h_part, block, 2 * block), h_far)
+    upstream_ring = lax.optimization_barrier((*upstream_ring, *late))[:4]
     turned = turn(upstream_ring)
     all_upstream = jnp.concatenate([turned, send(turned, SWAP_CORE)], axis=1)
     g_part = dot(all_upstream, w_out, (1, 1), (1024, 512, 256))
     g_far, sent = start_far(cut(g_part, 0, block))
-    hidden = finish_columns(after(cut(h_part, 2 * block, 3 * block), sent), h_near)
-    g_near = start_near(cut(g_part, block, 2 * block), cut(g_part, 2 * block, 3 * block), g_far)
+    g_parts, early, _ = start_near(cut(g_part, block, 2 * block), cut(g_part, 2 * block, 3 * block), g_far)
+    h_parts = lax.optimization_barrier((*h_parts, sent, *early))[:4]
+    hidden = finish_columns(cut(h_part, 2 * block, 3 * block), h_parts)
 
     act, slope = lax.optimization_barrier((narrow(gelu_value(hidden)), gelu_slope(hidden)))
     a_up, a_down = send(act, X_DOWN), send(act, X_UP)
-    grad_act = finish_columns(after(cut(g_part, 3 * block, 4 * block), act), g_near)
+    g_parts = lax.optimization_barrier((*g_parts, act))[:4]
+    grad_act = finish_columns(cut(g_part, 3 * block, 4 * block), g_parts)
     a_low, a_high = gather_far(a_up, a_down)
     grad_hidden = narrow(grad_act * slope)
     b_up, b_down = send(grad_hidden, X_DOWN), send(grad_hidden, X_UP)
@@ -239,12 +245,11 @@
     part = dot(all_tokens, all_grad, (0, 0), (512, 1024, 256), jnp.bfloat16)
     in_part, other = halves(part, 0)
     in_received = send(other, SWAP_CORE)
-    out_received = after(out_received, part)
+    r_mine, r_received, r_other = finish_rows(after(own, part), parts)
+
+    output = narrow(o_mine + o_received)
+    out_received, in_received = lax.optimization_barrier((out_received, in_received, r_other))[:2]
     grad_weight_out = ordered(c, out_part, out_received, 0)
-    r_mine, r_received, r_other = finish_rows(after(own, part), parts)
-
-    output = narrow(o_mine + o_received)
-    in_received = after(in_received, r_other)
     grad_weight_in = ordered(c, in_part, in_received, 1)
     grad_tokens = narrow(r_mine + r_received)
     return (output, grad_tokens, grad_weight_in, grad_weight_out)

time: 274 us -> 299 us (1.091)
  starting transfers between devices: 55.9 us -> 68.7 us
  waiting for transfers between devices: 118 us -> 122 us
  other arithmetic: 35.1 us -> 38.8 us
  local copies, waits for them, and re-layouts: 20.3 us -> 23.3 us
    ppermute x44 -> x51, starting transfers between devices: 55.9 us -> 68.7 us  [send(): return lax.ppermute(value, ('row', 'col'), pairs)]
    ppermute x44 -> x51, waiting for transfers between devices: 118 us -> 122 us  [send(): return lax.ppermute(value, ('row', 'col'), pairs)]
    convert_element_type x10 -> x8, other arithmetic: 11.1 us -> 7 us  [narrow(): return value.astype(jnp.bfloat16)]
    unnamed x63 -> x65, local copies, waits for them, and re-layouts: 10.8 us -> 13.6 us
  transfers between devices with their start and end apart: 44 -> 51, of which waited for: 19 -> 17; matrix products, arithmetic and copies ran while one was open for 16% -> 14% of each run, Pallas kernels for 16% -> 14%
where the time goes in v1:
time: 299 us; the launch traced here: 297 us
  waiting for transfers between devices  122 us (41%)
  starting transfers between devices  68.7 us (23%)
  Pallas kernels  42.9 us (14%)
  other arithmetic  38.8 us (13%)
  local copies, waits for them, and re-layouts  23.3 us (8%)
    ppermute x51, waiting for transfers between devices, send(): return lax.ppermute(value, ('row', 'col'), pairs)  122 us
    ppermute x51, starting transfers between devices, send(): return lax.ppermute(value, ('row', 'col'), pairs)  68.7 us
    pallas_call x9, Pallas kernels, dot(): pl.pallas_call(kernel, grid=(tall // rows, wide // columns), in_specs=[le...  42.9 us
    unnamed x65, local copies, waits for them, and re-layouts  13.6 us
    convert_element_type x8, other arithmetic, narrow(): return value.astype(jnp.bfloat16)  7 us
  transfers between devices with their start and end apart: 51, of which 17 were waited for; matrix products, arithmetic and copies ran while one was open for 14% of the time, Pallas kernels for 14%

profile of v1, /device:TPU:0, one launch (start us, length us, event | category | flops | bytes accessed | tf_op | source)
XLA Modules:
  0.0 297.3 jit_solution(706979108545492552)
XLA Ops:
  0.6 3.4 %collective-permute-start = (bf16[128,512]{1,0:T(8,128)(2,1)}, bf16[128,512]{1,0:T(8,128)(2,1)S(1)}, u32[]{:S(2)}, u32[]{:S(2)}) collective-permute-start(bf16[128,512]{1,0:T(8,128)(2,1)} %param.4), channel_id=1, source_target_pairs={{0,16},{1,17},{2,18},{3,19},{4,20},{5,21},{6,22},{7,23},{8,24},{9,... | collective-permute-start | bytes 393224 | tf_op jit(solution)/shard_map/ppermute | solution.py:43
  4.0 4.0 %collective-permute-start.1 = (bf16[128,512]{1,0:T(8,128)(2,1)}, bf16[128,512]{1,0:T(8,128)(2,1)S(1)}, u32[]{:S(2)}, u32[]{:S(2)}) collective-permute-start(bf16[128,512]{1,0:T(8,128)(2,1)} %param.4), channel_id=1, source_target_pairs={{0,96},{1,97},{2,98},{3,99},{4,100},{5,101},{6,102},{7,103},{8,104... | collective-permute-start | bytes 393224 | tf_op jit(solution)/shard_map/ppermute | solution.py:43
  9.3 4.5 %broadcast_select_fusion.7 = (bf16[512,2048]{1,0:T(8,128)(2,1)}, bf16[512,2048]{1,0:T(8,128)(2,1)}) fusion(pred[]{:T(512)S(6)} %eq.60, bf16[512,4096]{1,0:T(8,128)(2,1)} %param.5), kind=kLoop, calls=%fused_computation.30 | loop fusion | flops 2097152 | bytes 8388609 | tf_op jit(solution)/shard_map/jit(_where)/select_n | solution.py:122
  14.0 2.0 collective-permute-start.2
  16.1 2.4 collective-permute-start.4
  18.5 2.2 collective-permute-done.2
  20.6 4.4 %collective-permute-start.6 = (bf16[128,512]{1,0:T(8,128)(2,1)S(1)}, bf16[128,512]{1,0:T(8,128)(2,1)S(1)}, u32[]{:S(2)}, u32[]{:S(2)}) collective-permute-start(bf16[128,512]{1,0:T(8,128)(2,1)S(1)} %collective-permute-done), channel_id=1, source_target_pairs={{0,32},{1,33},{2,34},{3,35},{4,36},{5,37},{6,38},{7,39},{8,40},{9,... | collective-permute-start | bytes 393224 | tf_op jit(solution)/shard_map/ppermute | solution.py:43
  25.1 2.4 collective-permute-done.6
  31.7 2.2 pad_maximum_fusion.right_ref
  33.9 2.3 shard_map.75
  36.4 1.6 collective-permute-start.11
  38.0 1.7 collective-permute-start.13
  40.6 3.7 %collective-permute-start.17 = (bf16[256,512]{1,0:T(8,128)(2,1)S(1)}, bf16[256,512]{1,0:T(8,128)(2,1)S(1)}, u32[]{:S(2)}, u32[]{:S(2)}) collective-permute-start(bf16[256,512]{1,0:T(8,128)(2,1)S(1)} %constant_dynamic-update-slice_fusion.8), channel_id=1, source_target_pairs={{0,64},{1,65},{2,66},{3,67},{4,68},{5,69},{6,70},{7,71},{8,72},{9,... | collective-permute-start | bytes 786440 | tf_op jit(solution)/shard_map/ppermute | solution.py:43
  44.5 6.0 %shard_map.76 = f32[768,2048]{1,0:T(8,128)S(1)} custom-call(bf16[768,1024]{1,0:T(8,128)(2,1)S(1)} %slice.194.left_ref, bf16[1024,2048]{1,0:T(8,128)(2,1)S(1)} %pad_maximum_fusion.right_ref), custom_call_target="tpu_custom_call" | custom-call | flops 3221225472 | bytes 12058624 | tf_op jit(solution)/shard_map/pallas_call | solution.py:87
  50.9 2.4 collective-permute-start.18
  54.6 4.2 %collective-permute-done.18 = bf16[256,512]{1,0:T(8,128)(2,1)S(1)} collective-permute-done((bf16[256,512]{1,0:T(8,128)(2,1)S(1)}, bf16[256,512]{1,0:T(8,128)(2,1)S(1)}, u32[]{:S(2)}, u32[]{:S(2)}) %collective-permute-start.18) | collective-permute-done | bytes 262176 | tf_op jit(solution)/shard_map/ppermute | solution.py:43
  60.7 1.5 collective-permute-start.10
  62.7 1.3 copy-done.21
  64.0 2.1 pad_maximum_fusion.1.right_ref
  66.5 3.0 %collective-permute-start.14 = (bf16[128,2048]{1,0:T(8,128)(2,1)}, bf16[128,2048]{1,0:T(8,128)(2,1)}, u32[]{:S(2)}, u32[]{:S(2)}) collective-permute-start(bf16[128,2048]{1,0:T(8,128)(2,1)} %get-tuple-element.64), channel_id=1, source_target_pairs={{0,12},{1,13},{2,14},{3,15},{4,0},{5,1},{6,2},{7,3},{8,4},{9,5},{1... | collective-permute-start | bytes 1572872 | tf_op jit(solution)/shard_map/ppermute | solution.py:43
  69.7 8.2 %shard_map.77 = f32[1024,2048]{1,0:T(8,128)S(1)} custom-call(bf16[1024,1024]{1,0:T(8,128)(2,1)S(1)} %pad_maximum_fusion.9.left_ref.right_ref, bf16[2048,1024]{1,0:T(8,128)(2,1)S(1)} %pad_maximum_fusion.1.right_ref), custom_call_target="tpu_custom_call" | custom-call | flops 4294967296 | bytes 14680064 | tf_op jit(solution)/shard_map/pallas_call | solution.py:87
  78.0 1.3 copy-done.9
  80.3 3.2 %collective-permute-start.29 = (bf16[128,2048]{1,0:T(8,128)(2,1)S(1)}, bf16[128,2048]{1,0:T(8,128)(2,1)S(1)}, u32[]{:S(2)}, u32[]{:S(2)}) collective-permute-start(bf16[128,2048]{1,0:T(8,128)(2,1)S(1)} %get-tuple-element.66), channel_id=1, source_target_pairs={{0,12},{1,13},{2,14},{3,15},{4,0},{5,1},{6,2},{7,3},{8,4},{9,5},{1... | collective-permute-start | bytes 1572872 | tf_op jit(solution)/shard_map/ppermute | solution.py:43
  83.5 6.3 %collective-permute-done.12 = bf16[128,2048]{1,0:T(8,128)(2,1)} collective-permute-done((bf16[128,2048]{1,0:T(8,128)(2,1)}, bf16[128,2048]{1,0:T(8,128)(2,1)}, u32[]{:S(2)}, u32[]{:S(2)}) %collective-permute-start.12) | collective-permute-done | bytes 524320 | tf_op jit(solution)/shard_map/ppermute | solution.py:43
  89.8 1.7 fusion.13
  92.7 3.2 %collective-permute-start.26 = (bf16[128,2048]{1,0:T(8,128)(2,1)S(1)}, bf16[128,2048]{1,0:T(8,128)(2,1)S(1)}, u32[]{:S(2)}, u32[]{:S(2)}) collective-permute-start(bf16[128,2048]{1,0:T(8,128)(2,1)S(1)} %get-tuple-element.67), channel_id=1, source_target_pairs={{0,12},{1,13},{2,14},{3,15},{4,0},{5,1},{6,2},{7,3},{8,4},{9,5},{1... | collective-permute-start | bytes 1572872 | tf_op jit(solution)/shard_map/ppermute | solution.py:43
  96.0 4.9 %collective-permute-done.27 = bf16[128,2048]{1,0:T(8,128)(2,1)S(1)} collective-permute-done((bf16[128,2048]{1,0:T(8,128)(2,1)S(1)}, bf16[128,2048]{1,0:T(8,128)(2,1)S(1)}, u32[]{:S(2)}, u32[]{:S(2)}) %collective-permute-start.27) | collective-permute-done | bytes 524320 | tf_op jit(solution)/shard_map/ppermute | solution.py:43
  101.3 3.2 %collective-permute-start.30 = (bf16[128,2048]{1,0:T(8,128)(2,1)S(1)}, bf16[128,2048]{1,0:T(8,128)(2,1)S(1)}, u32[]{:S(2)}, u32[]{:S(2)}) collective-permute-start(bf16[128,2048]{1,0:T(8,128)(2,1)S(1)} %get-tuple-element.56), channel_id=1, source_target_pairs={{0,12},{1,13},{2,14},{3,15},{4,0},{5,1},{6,2},{7,3},{8,4},{9,5},{1... | collective-permute-start | bytes 1572872 | tf_op jit(solution)/shard_map/ppermute | solution.py:43
  104.5 10.8 %collective-permute-done.21 = bf16[256,2048]{1,0:T(8,128)(2,1)S(1)} collective-permute-done((bf16[256,2048]{1,0:T(8,128)(2,1)S(1)}, bf16[256,2048]{1,0:T(8,128)(2,1)S(1)}, u32[]{:S(2)}, u32[]{:S(2)}) %collective-permute-start.21) | collective-permute-done | bytes 1048608 | tf_op jit(solution)/shard_map/ppermute | solution.py:43
  115.4 2.2 fusion.3
  117.6 5.0 %collective-permute-done.28 = bf16[128,2048]{1,0:T(8,128)(2,1)S(1)} collective-permute-done((bf16[128,2048]{1,0:T(8,128)(2,1)S(1)}, bf16[128,2048]{1,0:T(8,128)(2,1)S(1)}, u32[]{:S(2)}, u32[]{:S(2)}) %collective-permute-start.28) | collective-permute-done | bytes 524320 | tf_op jit(solution)/shard_map/ppermute | solution.py:43
  126.6 1.8 collective-permute-start.22
  128.3 21.7 %collective-permute-done.31 = bf16[256,2048]{1,0:T(8,128)(2,1)} collective-permute-done((bf16[256,2048]{1,0:T(8,128)(2,1)}, bf16[256,2048]{1,0:T(8,128)(2,1)}, u32[]{:S(2)}, u32[]{:S(2)}) %collective-permute-start.31) | collective-permute-done | bytes 1048608 | tf_op jit(solution)/shard_map/ppermute | solution.py:43
  150.0 2.6 multiply_convert_fusion
  153.3 1.5 collective-permute-start.39
  157.0 3.3 %collective-permute-start.32 = (bf16[128,2048]{1,0:T(8,128)(2,1)S(1)}, bf16[128,2048]{1,0:T(8,128)(2,1)S(1)}, u32[]{:S(2)}, u32[]{:S(2)}) collective-permute-start(bf16[128,2048]{1,0:T(8,128)(2,1)S(1)} %slice.214), channel_id=1, source_target_pairs={{0,12},{1,13},{2,14},{3,15},{4,0},{5,1},{6,2},{7,3},{8,4},{9,5},{1... | collective-permute-start | bytes 1572872 | tf_op jit(solution)/shard_map/ppermute | solution.py:43
  160.3 2.0 pad_maximum_fusion.6.left_ref
  162.4 4.8 %shard_map.78 = f32[768,1024]{1,0:T(8,128)S(1)} custom-call(bf16[768,2048]{1,0:T(8,128)(2,1)S(1)} %pad_maximum_fusion.6.left_ref, bf16[2048,1024]{1,0:T(8,128)(2,1)S(1)} %copy-done.3), custom_call_target="tpu_custom_call" | custom-call | flops 3221225472 | bytes 10485760 | tf_op jit(solution)/shard_map/pallas_call | solution.py:87
  167.4 21.9 %collective-permute-done.23 = bf16[128,2048]{1,0:T(8,128)(2,1)S(1)} collective-permute-done((bf16[128,2048]{1,0:T(8,128)(2,1)S(1)}, bf16[128,2048]{1,0:T(8,128)(2,1)S(1)}, u32[]{:S(2)}, u32[]{:S(2)}) %collective-permute-start.23) | collective-permute-done | bytes 524320 | tf_op jit(solution)/shard_map/ppermute | solution.py:43
  189.4 1.8 shard_map.79
  191.6 2.3 pad_maximum_fusion.2.left_ref
  193.9 6.3 %shard_map.80 = bf16[2048,1024]{1,0:T(8,128)(2,1)S(1)} custom-call(bf16[1024,2048]{1,0:T(8,128)(2,1)S(1)} %pad_maximum_fusion.2.left_ref, bf16[1024,1024]{1,0:T(8,128)(2,1)S(1)} %copy-done.10), custom_call_target="tpu_custom_call" | custom-call | flops 4294967296 | bytes 10485760 | tf_op jit(solution)/shard_map/pallas_call | solution.py:87
  200.3 1.7 slice.217
  203.4 2.4 copy-done.1
  205.9 4.7 %shard_map.81 = f32[768,1024]{1,0:T(8,128)S(1)} custom-call(bf16[768,2048]{1,0:T(8,128)(2,1)S(1)} %pad_maximum_fusion.7.left_ref, bf16[1024,2048]{1,0:T(8,128)(2,1)S(1)} %copy-done.1), custom_call_target="tpu_custom_call" | custom-call | flops 3221225472 | bytes 10485760 | tf_op jit(solution)/shard_map/pallas_call | solution.py:87
  210.6 1.5 slice.222
  214.8 3.0 %collective-permute-start.42 = (bf16[128,2048]{1,0:T(8,128)(2,1)S(1)}, bf16[128,2048]{1,0:T(8,128)(2,1)S(1)}, u32[]{:S(2)}, u32[]{:S(2)}) collective-permute-start(bf16[128,2048]{1,0:T(8,128)(2,1)S(1)} %slice.185), channel_id=1, source_target_pairs={{0,12},{1,13},{2,14},{3,15},{4,0},{5,1},{6,2},{7,3},{8,4},{9,5},{1... | collective-permute-start | bytes 1572872 | tf_op jit(solution)/shard_map/ppermute | solution.py:43
  217.8 10.3 %collective-permute-done.40 = bf16[128,2048]{1,0:T(8,128)(2,1)S(1)} collective-permute-done((bf16[128,2048]{1,0:T(8,128)(2,1)S(1)}, bf16[128,2048]{1,0:T(8,128)(2,1)S(1)}, u32[]{:S(2)}, u32[]{:S(2)}) %collective-permute-start.40) | collective-permute-done | bytes 524320 | tf_op jit(solution)/shard_map/ppermute | solution.py:43
  228.1 1.5 collective-permute-done.42
  229.7 1.6 shard_map.82
  233.6 2.2 slice_add_fusion
  239.4 7.1 %shard_map.83 = bf16[1024,2048]{1,0:T(8,128)(2,1)S(1)} custom-call(bf16[1024,1024]{1,0:T(8,128)(2,1)S(1)} %pad_maximum_fusion.8.left_ref, bf16[1024,2048]{1,0:T(8,128)(2,1)S(1)} %pad_maximum_fusion.3.right_ref), custom_call_target="tpu_custom_call" | custom-call | flops 4294967296 | bytes 10485760 | tf_op jit(solution)/shard_map/pallas_call | solution.py:87
  247.5 1.3 collective-permute-start.35
  249.2 2.6 collective-permute-start.37
  251.7 10.9 %collective-permute-done.35 = bf16[256,512]{1,0:T(8,128)(2,1)S(1)} collective-permute-done((bf16[256,512]{1,0:T(8,128)(2,1)S(1)}, bf16[256,512]{1,0:T(8,128)(2,1)S(1)}, u32[]{:S(2)}, u32[]{:S(2)}) %collective-permute-start.35) | collective-permute-done | bytes 262176 | tf_op jit(solution)/shard_map/ppermute | solution.py:43
  262.6 1.7 collective-permute-start.46
  264.3 1.6 collective-permute-start.47
  265.9 1.3 convert_add_fusion.2
  267.3 9.4 %collective-permute-done.45 = bf16[256,512]{1,0:T(8,128)(2,1)S(1)} collective-permute-done((bf16[256,512]{1,0:T(8,128)(2,1)S(1)}, bf16[256,512]{1,0:T(8,128)(2,1)S(1)}, u32[]{:S(2)}, u32[]{:S(2)}) %collective-permute-start.45) | collective-permute-done | bytes 262176 | tf_op jit(solution)/shard_map/ppermute | solution.py:43
  276.7 2.8 collective-permute-start.38
  280.4 6.9 %collective-permute-done.38 = f32[128,512]{1,0:T(8,128)S(1)} collective-permute-done((f32[128,512]{1,0:T(8,128)S(1)}, f32[128,512]{1,0:T(8,128)S(1)}, u32[]{:S(2)}, u32[]{:S(2)}) %collective-permute-start.38) | collective-permute-done | bytes 262176 | tf_op jit(solution)/shard_map/ppermute | solution.py:43
  288.0 2.9 collective-permute-done.48
  292.5 2.3 pad_maximum_fusion.5
  294.8 2.5 pad_maximum_fusion.4
  (176 shorter events, 35.9 us)
Async XLA Ops:
  0.6 13.4 %collective-permute-start = (bf16[128,512]{1,0:T(8,128)(2,1)}, bf16[128,512]{1,0:T(8,128)(2,1)S(1)}, u32[]{:S(2)}, u32[]{:S(2)}) collective-permute-start(bf16[128,512]{1,0:T(8,128)(2,1)} %param.4), channel_id=1, source_target_pairs={{0,16},{1,17},{2,18},{3,19},{4,20},{5,21},{6,22},{7,23},{8,24},{9,... | collective-permute-start | bytes 393224 | tf_op jit(solution)/shard_map/ppermute | solution.py:43
  4.0 12.0 %collective-permute-start.1 = (bf16[128,512]{1,0:T(8,128)(2,1)}, bf16[128,512]{1,0:T(8,128)(2,1)S(1)}, u32[]{:S(2)}, u32[]{:S(2)}) collective-permute-start(bf16[128,512]{1,0:T(8,128)(2,1)} %param.4), channel_id=1, source_target_pairs={{0,96},{1,97},{2,98},{3,99},{4,100},{5,101},{6,102},{7,103},{8,104... | collective-permute-start | bytes 393224 | tf_op jit(solution)/shard_map/ppermute | solution.py:43
  8.1 17.0 %collective-permute-start.3 = (bf16[128,512]{1,0:T(8,128)(2,1)}, bf16[128,512]{1,0:T(8,128)(2,1)S(1)}, u32[]{:S(2)}, u32[]{:S(2)}) collective-permute-start(bf16[128,512]{1,0:T(8,128)(2,1)} %param.4), channel_id=1, source_target_pairs={{0,64},{1,65},{2,66},{3,67},{4,68},{5,69},{6,70},{7,71},{8,72},{9,... | collective-permute-start | bytes 393224 | tf_op jit(solution)/shard_map/ppermute | solution.py:43
  8.1 17.0 %collective-permute-start.5 = (bf16[128,512]{1,0:T(8,128)(2,1)}, bf16[128,512]{1,0:T(8,128)(2,1)S(1)}, u32[]{:S(2)}, u32[]{:S(2)}) collective-permute-start(bf16[128,512]{1,0:T(8,128)(2,1)} %param.4), channel_id=1, source_target_pairs={{0,32},{1,33},{2,34},{3,35},{4,36},{5,37},{6,38},{7,39},{8,40},{9,... | collective-permute-start | bytes 393224 | tf_op jit(solution)/shard_map/ppermute | solution.py:43
  9.3 4.5 %copy-start.24 = (bf16[128,512]{1,0:T(8,128)(2,1)S(1)}, bf16[128,512]{1,0:T(8,128)(2,1)}, u32[]{:S(2)}) copy-start(bf16[128,512]{1,0:T(8,128)(2,1)} %param.4) | copy-start | bytes 393220
  13.9 16.9 %collective-permute-start.8 = (bf16[512,2048]{1,0:T(8,128)(2,1)}, bf16[512,2048]{1,0:T(8,128)(2,1)}, u32[]{:S(2)}, u32[]{:S(2)}) collective-permute-start(bf16[512,2048]{1,0:T(8,128)(2,1)} %get-tuple-element.73), channel_id=1, source_target_pairs={{0,1},{1,0},{2,3},{3,2},{4,5},{5,4},{6,7},{7,6},{8,9},{9,8},{10,11... | collective-permute-start | bytes 6291464 | tf_op jit(solution)/shard_map/ppermute | solution.py:43
  14.0 6.6 %collective-permute-start.2 = (bf16[128,512]{1,0:T(8,128)(2,1)S(1)}, bf16[128,512]{1,0:T(8,128)(2,1)S(1)}, u32[]{:S(2)}, u32[]{:S(2)}) collective-permute-start(bf16[128,512]{1,0:T(8,128)(2,1)S(1)} %collective-permute-done), channel_id=1, source_target_pairs={{0,96},{1,97},{2,98},{3,99},{4,100},{5,101},{6,102},{7,103},{8,104... | collective-permute-start | bytes 393224 | tf_op jit(solution)/shard_map/ppermute | solution.py:43
  16.1 9.0 %collective-permute-start.4 = (bf16[128,512]{1,0:T(8,128)(2,1)S(1)}, bf16[128,512]{1,0:T(8,128)(2,1)S(1)}, u32[]{:S(2)}, u32[]{:S(2)}) collective-permute-start(bf16[128,512]{1,0:T(8,128)(2,1)S(1)} %collective-permute-done), channel_id=1, source_target_pairs={{0,64},{1,65},{2,66},{3,67},{4,68},{5,69},{6,70},{7,71},{8,72},{9,... | collective-permute-start | bytes 393224 | tf_op jit(solution)/shard_map/ppermute | solution.py:43
  20.6 6.9 %collective-permute-start.6 = (bf16[128,512]{1,0:T(8,128)(2,1)S(1)}, bf16[128,512]{1,0:T(8,128)(2,1)S(1)}, u32[]{:S(2)}, u32[]{:S(2)}) collective-permute-start(bf16[128,512]{1,0:T(8,128)(2,1)S(1)} %collective-permute-done), channel_id=1, source_target_pairs={{0,32},{1,33},{2,34},{3,35},{4,36},{5,37},{6,38},{7,39},{8,40},{9,... | collective-permute-start | bytes 393224 | tf_op jit(solution)/shard_map/ppermute | solution.py:43
  27.7 2.7 collective-permute-start.7
  28.4 11.3 %collective-permute-start.15 = (bf16[128,512]{1,0:T(8,128)(2,1)S(1)}, bf16[128,512]{1,0:T(8,128)(2,1)S(1)}, u32[]{:S(2)}, u32[]{:S(2)}) collective-permute-start(bf16[128,512]{1,0:T(8,128)(2,1)S(1)} %copy-done.25), channel_id=1, source_target_pairs={{0,16},{1,17},{2,18},{3,19},{4,20},{5,21},{6,22},{7,23},{8,24},{9,... | collective-permute-start | bytes 393224 | tf_op jit(solution)/shard_map/ppermute | solution.py:43
  30.1 32.6 %collective-permute-start.20 = (bf16[2048,512]{1,0:T(8,128)(2,1)S(1)}, bf16[2048,512]{1,0:T(8,128)(2,1)S(1)}, u32[]{:S(2)}, u32[]{:S(2)}) collective-permute-start(bf16[2048,512]{1,0:T(8,128)(2,1)S(1)} %get-tuple-element.71), channel_id=1, source_target_pairs={{0,1},{1,0},{2,3},{3,2},{4,5},{5,4},{6,7},{7,6},{8,9},{9,8},{10,11... | collective-permute-start | bytes 6291464 | tf_op jit(solution)/shard_map/ppermute | solution.py:43
  33.8 10.6 %copy-start = (bf16[1024,2048]{1,0:T(8,128)(2,1)}, bf16[1024,2048]{1,0:T(8,128)(2,1)S(1)}, u32[]{:S(2)}) copy-start(bf16[1024,2048]{1,0:T(8,128)(2,1)S(1)} %pad_maximum_fusion.right_ref) | copy-start | bytes 12582916
  36.4 14.5 %collective-permute-start.11 = (bf16[128,2048]{1,0:T(8,128)(2,1)S(1)}, bf16[128,2048]{1,0:T(8,128)(2,1)S(1)}, u32[]{:S(2)}, u32[]{:S(2)}) collective-permute-start(bf16[128,2048]{1,0:T(8,128)(2,1)S(1)} %get-tuple-element.91), channel_id=1, source_target_pairs={{0,4},{1,5},{2,6},{3,7},{4,8},{5,9},{6,10},{7,11},{8,12},{9,13},{1... | collective-permute-start | bytes 1572872 | tf_op jit(solution)/shard_map/ppermute | solution.py:43
  38.0 15.3 %collective-permute-start.13 = (bf16[128,2048]{1,0:T(8,128)(2,1)S(1)}, bf16[128,2048]{1,0:T(8,128)(2,1)S(1)}, u32[]{:S(2)}, u32[]{:S(2)}) collective-permute-start(bf16[128,2048]{1,0:T(8,128)(2,1)S(1)} %get-tuple-element.90), channel_id=1, source_target_pairs={{0,12},{1,13},{2,14},{3,15},{4,0},{5,1},{6,2},{7,3},{8,4},{9,5},{1... | collective-permute-start | bytes 1572872 | tf_op jit(solution)/shard_map/ppermute | solution.py:43
  39.8 14.8 %collective-permute-start.16 = (bf16[256,512]{1,0:T(8,128)(2,1)S(1)}, bf16[256,512]{1,0:T(8,128)(2,1)S(1)}, u32[]{:S(2)}, u32[]{:S(2)}) collective-permute-start(bf16[256,512]{1,0:T(8,128)(2,1)S(1)} %constant_dynamic-update-slice_fusion.8), channel_id=1, source_target_pairs={{0,96},{1,97},{2,98},{3,99},{4,100},{5,101},{6,102},{7,103},{8,104... | collective-permute-start | bytes 786440 | tf_op jit(solution)/shard_map/ppermute | solution.py:43
  40.6 14.0 %collective-permute-start.17 = (bf16[256,512]{1,0:T(8,128)(2,1)S(1)}, bf16[256,512]{1,0:T(8,128)(2,1)S(1)}, u32[]{:S(2)}, u32[]{:S(2)}) collective-permute-start(bf16[256,512]{1,0:T(8,128)(2,1)S(1)} %constant_dynamic-update-slice_fusion.8), channel_id=1, source_target_pairs={{0,64},{1,65},{2,66},{3,67},{4,68},{5,69},{6,70},{7,71},{8,72},{9,... | collective-permute-start | bytes 786440 | tf_op jit(solution)/shard_map/ppermute | solution.py:43
  50.9 7.9 %collective-permute-start.18 = (bf16[256,512]{1,0:T(8,128)(2,1)S(1)}, bf16[256,512]{1,0:T(8,128)(2,1)S(1)}, u32[]{:S(2)}, u32[]{:S(2)}) collective-permute-start(bf16[256,512]{1,0:T(8,128)(2,1)S(1)} %constant_dynamic-update-slice_fusion.8), channel_id=1, source_target_pairs={{0,32},{1,33},{2,34},{3,35},{4,36},{5,37},{6,38},{7,39},{8,40},{9,... | collective-permute-start | bytes 786440 | tf_op jit(solution)/shard_map/ppermute | solution.py:43
  59.1 10.4 %collective-permute-start.19 = (bf16[1024,512]{1,0:T(8,128)(2,1)S(1)}, bf16[1024,512]{1,0:T(8,128)(2,1)S(1)}, u32[]{:S(2)}, u32[]{:S(2)}) collective-permute-start(bf16[1024,512]{1,0:T(8,128)(2,1)S(1)} %pad_maximum_fusion.15), channel_id=1, source_target_pairs={{0,1},{1,0},{2,3},{3,2},{4,5},{5,4},{6,7},{7,6},{8,9},{9,8},{10,11... | collective-permute-start | bytes 3145736 | tf_op jit(solution)/shard_map/ppermute | solution.py:43
  60.7 19.6 %collective-permute-start.10 = (bf16[128,2048]{1,0:T(8,128)(2,1)}, bf16[128,2048]{1,0:T(8,128)(2,1)S(1)}, u32[]{:S(2)}, u32[]{:S(2)}) collective-permute-start(bf16[128,2048]{1,0:T(8,128)(2,1)} %get-tuple-element.76), channel_id=1, source_target_pairs={{0,12},{1,13},{2,14},{3,15},{4,0},{5,1},{6,2},{7,3},{8,4},{9,5},{1... | collective-permute-start | bytes 1572872 | tf_op jit(solution)/shard_map/ppermute | solution.py:43
  62.2 21.3 %collective-permute-start.9 = (bf16[128,2048]{1,0:T(8,128)(2,1)}, bf16[128,2048]{1,0:T(8,128)(2,1)S(1)}, u32[]{:S(2)}, u32[]{:S(2)}) collective-permute-start(bf16[128,2048]{1,0:T(8,128)(2,1)} %get-tuple-element.77), channel_id=1, source_target_pairs={{0,4},{1,5},{2,6},{3,7},{4,8},{5,9},{6,10},{7,11},{8,12},{9,13},{1... | collective-permute-start | bytes 1572872 | tf_op jit(solution)/shard_map/ppermute | solution.py:43
  66.1 3.6 %copy-start.2 = (bf16[2048,1024]{1,0:T(8,128)(2,1)}, bf16[2048,1024]{1,0:T(8,128)(2,1)S(1)}, u32[]{:S(2)}) copy-start(bf16[2048,1024]{1,0:T(8,128)(2,1)S(1)} %pad_maximum_fusion.1.right_ref) | copy-start | bytes 12582916
  66.1 23.6 %collective-permute-start.12 = (bf16[128,2048]{1,0:T(8,128)(2,1)}, bf16[128,2048]{1,0:T(8,128)(2,1)}, u32[]{:S(2)}, u32[]{:S(2)}) collective-permute-start(bf16[128,2048]{1,0:T(8,128)(2,1)} %get-tuple-element.65), channel_id=1, source_target_pairs={{0,4},{1,5},{2,6},{3,7},{4,8},{5,9},{6,10},{7,11},{8,12},{9,13},{1... | collective-permute-start | bytes 1572872 | tf_op jit(solution)/shard_map/ppermute | solution.py:43
  66.5 23.3 %collective-permute-start.14 = (bf16[128,2048]{1,0:T(8,128)(2,1)}, bf16[128,2048]{1,0:T(8,128)(2,1)}, u32[]{:S(2)}, u32[]{:S(2)}) collective-permute-start(bf16[128,2048]{1,0:T(8,128)(2,1)} %get-tuple-element.64), channel_id=1, source_target_pairs={{0,12},{1,13},{2,14},{3,15},{4,0},{5,1},{6,2},{7,3},{8,4},{9,5},{1... | collective-permute-start | bytes 1572872 | tf_op jit(solution)/shard_map/ppermute | solution.py:43
  80.2 20.7 %collective-permute-start.27 = (bf16[128,2048]{1,0:T(8,128)(2,1)S(1)}, bf16[128,2048]{1,0:T(8,128)(2,1)S(1)}, u32[]{:S(2)}, u32[]{:S(2)}) collective-permute-start(bf16[128,2048]{1,0:T(8,128)(2,1)S(1)} %get-tuple-element.69), channel_id=1, source_target_pairs={{0,4},{1,5},{2,6},{3,7},{4,8},{5,9},{6,10},{7,11},{8,12},{9,13},{1... | collective-permute-start | bytes 1572872 | tf_op jit(solution)/shard_map/ppermute | solution.py:43
  80.3 20.6 %collective-permute-start.29 = (bf16[128,2048]{1,0:T(8,128)(2,1)S(1)}, bf16[128,2048]{1,0:T(8,128)(2,1)S(1)}, u32[]{:S(2)}, u32[]{:S(2)}) collective-permute-start(bf16[128,2048]{1,0:T(8,128)(2,1)S(1)} %get-tuple-element.66), channel_id=1, source_target_pairs={{0,12},{1,13},{2,14},{3,15},{4,0},{5,1},{6,2},{7,3},{8,4},{9,5},{1... | collective-permute-start | bytes 1572872 | tf_op jit(solution)/shard_map/ppermute | solution.py:43
  91.6 23.8 %collective-permute-start.21 = (bf16[256,2048]{1,0:T(8,128)(2,1)S(1)}, bf16[256,2048]{1,0:T(8,128)(2,1)S(1)}, u32[]{:S(2)}, u32[]{:S(2)}) collective-permute-start(bf16[256,2048]{1,0:T(8,128)(2,1)S(1)} %fusion.5), channel_id=1, source_target_pairs={{0,2},{1,3},{2,0},{3,1},{4,6},{5,7},{6,4},{7,5},{8,10},{9,11},{10,... | collective-permute-start | bytes 3145736 | tf_op jit(solution)/shard_map/ppermute | solution.py:43
  92.7 24.9 %collective-permute-start.25 = (bf16[128,2048]{1,0:T(8,128)(2,1)S(1)}, bf16[128,2048]{1,0:T(8,128)(2,1)S(1)}, u32[]{:S(2)}, u32[]{:S(2)}) collective-permute-start(bf16[128,2048]{1,0:T(8,128)(2,1)S(1)} %get-tuple-element.68), channel_id=1, source_target_pairs={{0,4},{1,5},{2,6},{3,7},{4,8},{5,9},{6,10},{7,11},{8,12},{9,13},{1... | collective-permute-start | bytes 1572872 | tf_op jit(solution)/shard_map/ppermute | solution.py:43
  92.7 24.9 %collective-permute-start.26 = (bf16[128,2048]{1,0:T(8,128)(2,1)S(1)}, bf16[128,2048]{1,0:T(8,128)(2,1)S(1)}, u32[]{:S(2)}, u32[]{:S(2)}) collective-permute-start(bf16[128,2048]{1,0:T(8,128)(2,1)S(1)} %get-tuple-element.67), channel_id=1, source_target_pairs={{0,12},{1,13},{2,14},{3,15},{4,0},{5,1},{6,2},{7,3},{8,4},{9,5},{1... | collective-permute-start | bytes 1572872 | tf_op jit(solution)/shard_map/ppermute | solution.py:43
  101.2 21.4 %collective-permute-start.28 = (bf16[128,2048]{1,0:T(8,128)(2,1)S(1)}, bf16[128,2048]{1,0:T(8,128)(2,1)S(1)}, u32[]{:S(2)}, u32[]{:S(2)}) collective-permute-start(bf16[128,2048]{1,0:T(8,128)(2,1)S(1)} %get-tuple-element.57), channel_id=1, source_target_pairs={{0,4},{1,5},{2,6},{3,7},{4,8},{5,9},{6,10},{7,11},{8,12},{9,13},{1... | collective-permute-start | bytes 1572872 | tf_op jit(solution)/shard_map/ppermute | solution.py:43
  101.3 21.3 %collective-permute-start.30 = (bf16[128,2048]{1,0:T(8,128)(2,1)S(1)}, bf16[128,2048]{1,0:T(8,128)(2,1)S(1)}, u32[]{:S(2)}, u32[]{:S(2)}) collective-permute-start(bf16[128,2048]{1,0:T(8,128)(2,1)S(1)} %get-tuple-element.56), channel_id=1, source_target_pairs={{0,12},{1,13},{2,14},{3,15},{4,0},{5,1},{6,2},{7,3},{8,4},{9,5},{1... | collective-permute-start | bytes 1572872 | tf_op jit(solution)/shard_map/ppermute | solution.py:43
  125.3 24.7 %collective-permute-start.31 = (bf16[256,2048]{1,0:T(8,128)(2,1)}, bf16[256,2048]{1,0:T(8,128)(2,1)}, u32[]{:S(2)}, u32[]{:S(2)}) collective-permute-start(bf16[256,2048]{1,0:T(8,128)(2,1)} %fusion.4), channel_id=1, source_target_pairs={{0,2},{1,3},{2,0},{3,1},{4,6},{5,7},{6,4},{7,5},{8,10},{9,11},{10,... | collective-permute-start | bytes 3145736 | tf_op jit(solution)/shard_map/ppermute | solution.py:43
  126.3 28.5 %collective-permute-start.24 = (bf16[256,2048]{1,0:T(8,128)(2,1)}, bf16[256,2048]{1,0:T(8,128)(2,1)}, u32[]{:S(2)}, u32[]{:S(2)}) collective-permute-start(bf16[256,2048]{1,0:T(8,128)(2,1)} %get-tuple-element.38), channel_id=1, source_target_pairs={{0,12},{1,13},{2,14},{3,15},{4,0},{5,1},{6,2},{7,3},{8,4},{9,5},{1... | collective-permute-start | bytes 3145736 | tf_op jit(solution)/shard_map/ppermute | solution.py:43
  126.6 28.2 %collective-permute-start.22 = (bf16[256,2048]{1,0:T(8,128)(2,1)}, bf16[256,2048]{1,0:T(8,128)(2,1)}, u32[]{:S(2)}, u32[]{:S(2)}) collective-permute-start(bf16[256,2048]{1,0:T(8,128)(2,1)} %get-tuple-element.38), channel_id=1, source_target_pairs={{0,4},{1,5},{2,6},{3,7},{4,8},{5,9},{6,10},{7,11},{8,12},{9,13},{1... | collective-permute-start | bytes 3145736 | tf_op jit(solution)/shard_map/ppermute | solution.py:43
  152.7 50.3 %copy-start.12 = (bf16[256,2048]{1,0:T(8,128)(2,1)}, bf16[256,2048]{1,0:T(8,128)(2,1)S(1)}, u32[]{:S(2)}) copy-start(bf16[256,2048]{1,0:T(8,128)(2,1)S(1)} %multiply_convert_fusion) | copy-start | bytes 3145732
  152.7 50.3 %collective-permute-start.41 = (bf16[256,2048]{1,0:T(8,128)(2,1)S(1)}, bf16[256,2048]{1,0:T(8,128)(2,1)S(1)}, u32[]{:S(2)}, u32[]{:S(2)}) collective-permute-start(bf16[256,2048]{1,0:T(8,128)(2,1)S(1)} %multiply_convert_fusion), channel_id=1, source_target_pairs={{0,12},{1,13},{2,14},{3,15},{4,0},{5,1},{6,2},{7,3},{8,4},{9,5},{1... | collective-permute-start | bytes 3145736 | tf_op jit(solution)/shard_map/ppermute | solution.py:43
  153.3 49.6 %collective-permute-start.39 = (bf16[256,2048]{1,0:T(8,128)(2,1)S(1)}, bf16[256,2048]{1,0:T(8,128)(2,1)S(1)}, u32[]{:S(2)}, u32[]{:S(2)}) collective-permute-start(bf16[256,2048]{1,0:T(8,128)(2,1)S(1)} %multiply_convert_fusion), channel_id=1, source_target_pairs={{0,4},{1,5},{2,6},{3,7},{4,8},{5,9},{6,10},{7,11},{8,12},{9,13},{1... | collective-permute-start | bytes 3145736 | tf_op jit(solution)/shard_map/ppermute | solution.py:43
  155.9 33.5 %collective-permute-start.23 = (bf16[128,2048]{1,0:T(8,128)(2,1)S(1)}, bf16[128,2048]{1,0:T(8,128)(2,1)S(1)}, u32[]{:S(2)}, u32[]{:S(2)}) collective-permute-start(bf16[128,2048]{1,0:T(8,128)(2,1)S(1)} %slice.207), channel_id=1, source_target_pairs={{0,4},{1,5},{2,6},{3,7},{4,8},{5,9},{6,10},{7,11},{8,12},{9,13},{1... | collective-permute-start | bytes 1572872 | tf_op jit(solution)/shard_map/ppermute | solution.py:43
  157.0 5.3 %copy-start.3 = (bf16[2048,1024]{1,0:T(8,128)(2,1)S(1)}, bf16[2048,1024]{1,0:T(8,128)(2,1)}, u32[]{:S(2)}) copy-start(bf16[2048,1024]{1,0:T(8,128)(2,1)} %copy-done.2) | copy-start | bytes 12582916
  157.0 32.3 %collective-permute-start.32 = (bf16[128,2048]{1,0:T(8,128)(2,1)S(1)}, bf16[128,2048]{1,0:T(8,128)(2,1)S(1)}, u32[]{:S(2)}, u32[]{:S(2)}) collective-permute-start(bf16[128,2048]{1,0:T(8,128)(2,1)S(1)} %slice.214), channel_id=1, source_target_pairs={{0,12},{1,13},{2,14},{3,15},{4,0},{5,1},{6,2},{7,3},{8,4},{9,5},{1... | collective-permute-start | bytes 1572872 | tf_op jit(solution)/shard_map/ppermute | solution.py:43
  167.3 45.8 %collective-permute-start.34 = (f32[768,512]{1,0:T(8,128)S(1)}, f32[768,512]{1,0:T(8,128)S(1)}, u32[]{:S(2)}, u32[]{:S(2)}) collective-permute-start(f32[768,512]{1,0:T(8,128)S(1)} %slice.213), channel_id=1, source_target_pairs={{0,1},{1,0},{2,3},{3,2},{4,5},{5,4},{6,7},{7,6},{8,9},{9,8},{10,11... | collective-permute-start | bytes 4718600 | tf_op jit(solution)/shard_map/ppermute | solution.py:43
  191.3 2.6 copy-start.10
  191.3 21.8 %collective-permute-start.33 = (f32[256,512]{1,0:T(8,128)S(1)}, f32[256,512]{1,0:T(8,128)S(1)}, u32[]{:S(2)}, u32[]{:S(2)}) collective-permute-start(f32[256,512]{1,0:T(8,128)S(1)} %get-tuple-element.84), channel_id=1, source_target_pairs={{0,1},{1,0},{2,3},{3,2},{4,5},{5,4},{6,7},{7,6},{8,9},{9,8},{10,11... | collective-permute-start | bytes 1572872 | tf_op jit(solution)/shard_map/ppermute | solution.py:43
  200.3 2.6 copy-start.6
  202.9 2.9 copy-start.1
  202.9 11.8 %copy-start.15 = (bf16[256,2048]{1,0:T(8,128)(2,1)}, bf16[256,2048]{1,0:T(8,128)(2,1)S(1)}, u32[]{:S(2)}) copy-start(bf16[256,2048]{1,0:T(8,128)(2,1)S(1)} %collective-permute-done.41) | copy-start | bytes 3145732
  202.9 9.1 %copy-start.17 = (bf16[256,2048]{1,0:T(8,128)(2,1)}, bf16[256,2048]{1,0:T(8,128)(2,1)S(1)}, u32[]{:S(2)}) copy-start(bf16[256,2048]{1,0:T(8,128)(2,1)S(1)} %collective-permute-done.39) | copy-start | bytes 3145732
  212.7 15.4 %collective-permute-start.40 = (bf16[128,2048]{1,0:T(8,128)(2,1)S(1)}, bf16[128,2048]{1,0:T(8,128)(2,1)S(1)}, u32[]{:S(2)}, u32[]{:S(2)}) collective-permute-start(bf16[128,2048]{1,0:T(8,128)(2,1)S(1)} %slice.221), channel_id=1, source_target_pairs={{0,4},{1,5},{2,6},{3,7},{4,8},{5,9},{6,10},{7,11},{8,12},{9,13},{1... | collective-permute-start | bytes 1572872 | tf_op jit(solution)/shard_map/ppermute | solution.py:43
  212.7 20.9 %collective-permute-start.44 = (f32[768,512]{1,0:T(8,128)}, f32[768,512]{1,0:T(8,128)}, u32[]{:S(2)}, u32[]{:S(2)}) collective-permute-start(f32[768,512]{1,0:T(8,128)} %slice.222), channel_id=1, source_target_pairs={{0,1},{1,0},{2,3},{3,2},{4,5},{5,4},{6,7},{7,6},{8,9},{9,8},{10,11... | collective-permute-start | bytes 4718600 | tf_op jit(solution)/shard_map/ppermute | solution.py:43
  213.7 16.0 %copy-start.19 = (f32[1024,512]{1,0:T(8,128)}, f32[1024,512]{1,0:T(8,128)S(1)}, u32[]{:S(2)}) copy-start(f32[1024,512]{1,0:T(8,128)S(1)} %pad_maximum_fusion.12) | copy-start | bytes 6291460
  214.8 14.8 %collective-permute-start.42 = (bf16[128,2048]{1,0:T(8,128)(2,1)S(1)}, bf16[128,2048]{1,0:T(8,128)(2,1)S(1)}, u32[]{:S(2)}, u32[]{:S(2)}) collective-permute-start(bf16[128,2048]{1,0:T(8,128)(2,1)S(1)} %slice.185), channel_id=1, source_target_pairs={{0,12},{1,13},{2,14},{3,15},{4,0},{5,1},{6,2},{7,3},{8,4},{9,5},{1... | collective-permute-start | bytes 1572872 | tf_op jit(solution)/shard_map/ppermute | solution.py:43
  233.1 2.7 collective-permute-start.43
  233.1 2.8 copy-start.5
  233.1 58.6 %collective-permute-start.49 = (bf16[2048,512]{1,0:T(8,128)(2,1)}, bf16[2048,512]{1,0:T(8,128)(2,1)S(1)}, u32[]{:S(2)}, u32[]{:S(2)}) collective-permute-start(bf16[2048,512]{1,0:T(8,128)(2,1)} %slice.217), channel_id=1, source_target_pairs={{0,1},{1,0},{2,3},{3,2},{4,5},{5,4},{6,7},{7,6},{8,9},{9,8},{10,11... | collective-permute-start | bytes 6291464 | tf_op jit(solution)/shard_map/ppermute | solution.py:43
  246.7 45.0 %collective-permute-start.50 = (bf16[512,2048]{1,0:T(8,128)(2,1)S(1)}, bf16[512,2048]{1,0:T(8,128)(2,1)S(1)}, u32[]{:S(2)}, u32[]{:S(2)}) collective-permute-start(bf16[512,2048]{1,0:T(8,128)(2,1)S(1)} %slice.229), channel_id=1, source_target_pairs={{0,1},{1,0},{2,3},{3,2},{4,5},{5,4},{6,7},{7,6},{8,9},{9,8},{10,11... | collective-permute-start | bytes 6291464 | tf_op jit(solution)/shard_map/ppermute | solution.py:43
  247.5 15.1 %collective-permute-start.35 = (bf16[256,512]{1,0:T(8,128)(2,1)S(1)}, bf16[256,512]{1,0:T(8,128)(2,1)S(1)}, u32[]{:S(2)}, u32[]{:S(2)}) collective-permute-start(bf16[256,512]{1,0:T(8,128)(2,1)S(1)} %copy-done.23), channel_id=1, source_target_pairs={{0,32},{1,33},{2,34},{3,35},{4,36},{5,37},{6,38},{7,39},{8,40},{9,... | collective-permute-start | bytes 786440 | tf_op jit(solution)/shard_map/ppermute | solution.py:43
  248.8 13.8 %collective-permute-start.36 = (bf16[256,512]{1,0:T(8,128)(2,1)S(1)}, bf16[256,512]{1,0:T(8,128)(2,1)S(1)}, u32[]{:S(2)}, u32[]{:S(2)}) collective-permute-start(bf16[256,512]{1,0:T(8,128)(2,1)S(1)} %copy-done.22), channel_id=1, source_target_pairs={{0,64},{1,65},{2,66},{3,67},{4,68},{5,69},{6,70},{7,71},{8,72},{9,... | collective-permute-start | bytes 786440 | tf_op jit(solution)/shard_map/ppermute | solution.py:43
  249.2 15.1 %collective-permute-start.37 = (bf16[256,512]{1,0:T(8,128)(2,1)S(1)}, bf16[256,512]{1,0:T(8,128)(2,1)S(1)}, u32[]{:S(2)}, u32[]{:S(2)}) collective-permute-start(bf16[256,512]{1,0:T(8,128)(2,1)S(1)} %get-tuple-element.82), channel_id=1, source_target_pairs={{0,96},{1,97},{2,98},{3,99},{4,100},{5,101},{6,102},{7,103},{8,104... | collective-permute-start | bytes 786440 | tf_op jit(solution)/shard_map/ppermute | solution.py:43
  262.6 14.1 %collective-permute-start.45 = (bf16[256,512]{1,0:T(8,128)(2,1)S(1)}, bf16[256,512]{1,0:T(8,128)(2,1)S(1)}, u32[]{:S(2)}, u32[]{:S(2)}) collective-permute-start(bf16[256,512]{1,0:T(8,128)(2,1)S(1)} %get-tuple-element.78), channel_id=1, source_target_pairs={{0,32},{1,33},{2,34},{3,35},{4,36},{5,37},{6,38},{7,39},{8,40},{9,... | collective-permute-start | bytes 786440 | tf_op jit(solution)/shard_map/ppermute | solution.py:43
  262.6 16.8 %collective-permute-start.46 = (bf16[256,512]{1,0:T(8,128)(2,1)S(1)}, bf16[256,512]{1,0:T(8,128)(2,1)S(1)}, u32[]{:S(2)}, u32[]{:S(2)}) collective-permute-start(bf16[256,512]{1,0:T(8,128)(2,1)S(1)} %get-tuple-element.80), channel_id=1, source_target_pairs={{0,64},{1,65},{2,66},{3,67},{4,68},{5,69},{6,70},{7,71},{8,72},{9,... | collective-permute-start | bytes 786440 | tf_op jit(solution)/shard_map/ppermute | solution.py:43
  264.3 15.1 %collective-permute-start.47 = (bf16[256,512]{1,0:T(8,128)(2,1)S(1)}, bf16[256,512]{1,0:T(8,128)(2,1)S(1)}, u32[]{:S(2)}, u32[]{:S(2)}) collective-permute-start(bf16[256,512]{1,0:T(8,128)(2,1)S(1)} %get-tuple-element.79), channel_id=1, source_target_pairs={{0,96},{1,97},{2,98},{3,99},{4,100},{5,101},{6,102},{7,103},{8,104... | collective-permute-start | bytes 786440 | tf_op jit(solution)/shard_map/ppermute | solution.py:43
  265.9 25.8 %copy-start.7 = (bf16[2048,1024]{1,0:T(8,128)(2,1)S(1)}, bf16[2048,1024]{1,0:T(8,128)(2,1)}, u32[]{:S(2)}) copy-start(bf16[2048,1024]{1,0:T(8,128)(2,1)} %copy-done.6) | copy-start | bytes 12582916
  276.7 10.7 %collective-permute-start.38 = (f32[128,512]{1,0:T(8,128)S(1)}, f32[128,512]{1,0:T(8,128)S(1)}, u32[]{:S(2)}, u32[]{:S(2)}) collective-permute-start(f32[128,512]{1,0:T(8,128)S(1)} %slice.220), channel_id=1, source_target_pairs={{0,16},{1,17},{2,18},{3,19},{4,20},{5,21},{6,22},{7,23},{8,24},{9,... | collective-permute-start | bytes 786440 | tf_op jit(solution)/shard_map/ppermute | solution.py:43
  279.6 11.4 %collective-permute-start.48 = (f32[128,512]{1,0:T(8,128)S(1)}, f32[128,512]{1,0:T(8,128)S(1)}, u32[]{:S(2)}, u32[]{:S(2)}) collective-permute-start(f32[128,512]{1,0:T(8,128)S(1)} %slice.227), channel_id=1, source_target_pairs={{0,16},{1,17},{2,18},{3,19},{4,20},{5,21},{6,22},{7,23},{8,24},{9,... | collective-permute-start | bytes 786440 | tf_op jit(solution)/shard_map/ppermute | solution.py:43
  (13 other events, 19.1 us)

commit v2 on v1

--- a/solution.py
+++ b/solution.py
@@ -90,13 +90,39 @@
         in_specs=[left_spec, right_spec],
         out_specs=pl.BlockSpec((rows, columns), lambda i, j: (i, j)),
         out_shape=jax.ShapeDtypeStruct((tall, wide), dtype),
-        compiler_params=pltpu.CompilerParams(vmem_limit_bytes=16 << 20),
+        compiler_params=pltpu.CompilerParams(vmem_limit_bytes=12 << 20),
         cost_estimate=pl.CostEstimate(
             flops=2 * deep * tall * wide,
             transcendentals=0,
             bytes_accessed=2 * deep * (tall + wide) + item * tall * wide,
         ),
     )(left, right)
+
+
+def joined_dot(left, right, tiles):
+    tall, wide = left[0].shape[1], right[0].shape[1]
+    rows, columns = tiles
+
+    def kernel(*refs):
+        parts = [ref[...] for ref in refs[:-1]]
+        left_part = jnp.concatenate(parts[: len(left)], axis=0)
+        right_part = jnp.concatenate(parts[len(left) :], axis=0)
+        refs[-1][...] = lax.dot_general(
+            left_part, right_part, (((0,), (0,)), ((), ())), preferred_element_type=jnp.float32
+        ).astype(jnp.bfloat16)
+
+    return pl.pallas_call(
+        kernel,
+        grid=(wide // columns, tall // rows),
+        in_specs=[pl.BlockSpec((v.shape[0], rows), lambda j, i: (0, i)) for v in left]
+        + [pl.BlockSpec((v.shape[0], columns), lambda j, i: (0, j)) for v in right],
+        out_specs=pl.BlockSpec((rows, columns), lambda j, i: (i, j)),
+        out_shape=jax.ShapeDtypeStruct((tall, wide), jnp.bfloat16),
+        compiler_params=pltpu.CompilerParams(vmem_limit_bytes=12 << 20),
+        cost_estimate=pl.CostEstimate(
+            flops=2048 * tall * wide, transcendentals=0, bytes_accessed=2048 * (tall + wide)
+        ),
+    )(*left, *right)
 
 
 def narrow(value):
@@ -183,7 +209,7 @@
         return chunks[0], [narrow(v) for v in chunks[1:]]
 
     def finish_rows(own, parts):
-        parts = [send(v, row_move(k)) for k, v in zip((1, 2, 3), parts)]
+        parts = [send(v, row_move(k + 1)) for k, v in enumerate(parts)]
         mine, other = halves(own + parts[0] + parts[1] + parts[2], 0)
         return mine, send(other, SWAP_HI), other
 
@@ -221,7 +247,7 @@
     b_up, b_down = send(grad_hidden, X_DOWN), send(grad_hidden, X_UP)
 
     act_near = jnp.concatenate([after(a_up, grad_hidden), a_down, act], axis=0)
-    mine, other = halves(dot(act_near, w_out, (1, 0), (768, 512, 256)), 1)
+    mine, other = halves(dot(act_near, w_out, (1, 0), (768, 256, 256)), 1)
     near = mine, send(other, SWAP_CORE)
     act_far = jnp.concatenate([after(a_low, other), a_high], axis=0)
     mine, other = halves(dot(act_far, w_out, (1, 0), (256, 512, 256)), 1)
@@ -235,14 +261,13 @@
     b_low, b_high = gather_far(after(b_up, *parts), b_down)
 
     grad_near = jnp.concatenate([b_up, b_down, grad_hidden], axis=0)
-    mine, other = halves(dot(grad_near, w_in, (1, 1), (768, 512, 256)), 1)
+    mine, other = halves(dot(grad_near, w_in, (1, 1), (768, 256, 256)), 1)
     near = mine, send(other, SWAP_CORE)
     grad_far = jnp.concatenate([after(b_low, other), b_high], axis=0)
     mine, other = halves(dot(grad_far, w_in, (1, 1), (256, 512, 256)), 1)
     far = mine, send(other, SWAP_CORE)
     own, parts = split_rows(*far, *near)
-    all_grad = jnp.concatenate([after(grad_far, own, *parts), grad_near], axis=0)
-    part = dot(all_tokens, all_grad, (0, 0), (512, 1024, 256), jnp.bfloat16)
+    part = joined_dot((all_tokens,), (after(grad_far, own, *parts), grad_near), (512, 1024))
     in_part, other = halves(part, 0)
     in_received = send(other, SWAP_CORE)
     r_mine, r_received, r_other = finish_rows(after(own, part), parts)

time: 299 us -> 297 us (level)
    pallas_call x0 -> x1, Pallas kernels: none -> 5.99 us  [joined_dot(): pl.pallas_call(kernel, grid=(wide // columns, tall // rows), in_specs=[pl...]
    pallas_call x9 -> x8, Pallas kernels: 42.9 us -> 38.4 us  [dot(): pl.pallas_call(kernel, grid=(tall // rows, wide // columns), in_specs=[le...]
    unnamed x65 -> x57, local copies, waits for them, and re-layouts: 13.6 us -> 12.3 us
  transfers between devices with their start and end apart: 51 -> 51, of which waited for: 17 -> 17; matrix products, arithmetic and copies ran while one was open for 14% -> 14% of each run, Pallas kernels for 14% -> 15%
where the time goes in v2:
time: 297 us; the launch traced here: 295 us
  waiting for transfers between devices  120 us (40%)
  starting transfers between devices  68.7 us (23%)
  Pallas kernels  44.4 us (15%)
  other arithmetic  38.4 us (13%)
  local copies, waits for them, and re-layouts  22.1 us (7%)
    ppermute x51, waiting for transfers between devices, send(): return lax.ppermute(value, ('row', 'col'), pairs)  120 us
    ppermute x51, starting transfers between devices, send(): return lax.ppermute(value, ('row', 'col'), pairs)  68.7 us
    pallas_call x8, Pallas kernels, dot(): pl.pallas_call(kernel, grid=(tall // rows, wide // columns), in_specs=[le...  38.4 us
    unnamed x57, local copies, waits for them, and re-layouts  12.3 us
    convert_element_type x8, other arithmetic, narrow(): return value.astype(jnp.bfloat16)  7.07 us
    slice x12, local copies, waits for them, and re-layouts, halves(): lax.slice_in_dim(value, size, 2 * size, axis=axis)  6.01 us
    pallas_call x1, Pallas kernels, joined_dot(): pl.pallas_call(kernel, grid=(wide // columns, tall // rows), in_specs=[pl...  5.99 us
  transfers between devices with their start and end apart: 51, of which 17 were waited for; matrix products, arithmetic and copies ran while one was open for 14% of the time, Pallas kernels for 15%

profile of v2, /device:TPU:0, one launch (start us, length us, event | category | flops | bytes accessed | tf_op | source)
XLA Modules:
  0.0 295.2 jit_solution(11577298365703567903)
XLA Ops:
  0.6 3.4 %collective-permute-start = (bf16[128,512]{1,0:T(8,128)(2,1)}, bf16[128,512]{1,0:T(8,128)(2,1)S(1)}, u32[]{:S(2)}, u32[]{:S(2)}) collective-permute-start(bf16[128,512]{1,0:T(8,128)(2,1)} %param.4), channel_id=1, source_target_pairs={{0,16},{1,17},{2,18},{3,19},{4,20},{5,21},{6,22},{7,23},{8,24},{9,... | collective-permute-start | bytes 393224 | tf_op jit(solution)/shard_map/ppermute | solution.py:43
  4.0 4.0 %collective-permute-start.1 = (bf16[128,512]{1,0:T(8,128)(2,1)}, bf16[128,512]{1,0:T(8,128)(2,1)S(1)}, u32[]{:S(2)}, u32[]{:S(2)}) collective-permute-start(bf16[128,512]{1,0:T(8,128)(2,1)} %param.4), channel_id=1, source_target_pairs={{0,96},{1,97},{2,98},{3,99},{4,100},{5,101},{6,102},{7,103},{8,104... | collective-permute-start | bytes 393224 | tf_op jit(solution)/shard_map/ppermute | solution.py:43
  9.3 4.5 %broadcast_select_fusion.7 = (bf16[512,2048]{1,0:T(8,128)(2,1)}, bf16[512,2048]{1,0:T(8,128)(2,1)}) fusion(pred[]{:T(512)S(6)} %eq.60, bf16[512,4096]{1,0:T(8,128)(2,1)} %param.5), kind=kLoop, calls=%fused_computation.29 | loop fusion | flops 2097152 | bytes 8388609 | tf_op jit(solution)/shard_map/jit(_where)/select_n | solution.py:148
  14.0 2.0 collective-permute-start.2
  16.1 2.4 collective-permute-start.4
  18.5 2.2 collective-permute-done.2
  20.6 4.4 %collective-permute-start.6 = (bf16[128,512]{1,0:T(8,128)(2,1)S(1)}, bf16[128,512]{1,0:T(8,128)(2,1)S(1)}, u32[]{:S(2)}, u32[]{:S(2)}) collective-permute-start(bf16[128,512]{1,0:T(8,128)(2,1)S(1)} %collective-permute-done), channel_id=1, source_target_pairs={{0,32},{1,33},{2,34},{3,35},{4,36},{5,37},{6,38},{7,39},{8,40},{9,... | collective-permute-start | bytes 393224 | tf_op jit(solution)/shard_map/ppermute | solution.py:43
  25.1 2.4 collective-permute-done.6
  31.7 2.2 pad_maximum_fusion.right_ref
  33.9 2.3 shard_map.75
  36.4 1.6 collective-permute-start.11
  38.0 1.7 collective-permute-start.13
  40.6 3.7 %collective-permute-start.17 = (bf16[256,512]{1,0:T(8,128)(2,1)S(1)}, bf16[256,512]{1,0:T(8,128)(2,1)S(1)}, u32[]{:S(2)}, u32[]{:S(2)}) collective-permute-start(bf16[256,512]{1,0:T(8,128)(2,1)S(1)} %constant_dynamic-update-slice_fusion.8), channel_id=1, source_target_pairs={{0,64},{1,65},{2,66},{3,67},{4,68},{5,69},{6,70},{7,71},{8,72},{9,... | collective-permute-start | bytes 786440 | tf_op jit(solution)/shard_map/ppermute | solution.py:43
  44.5 6.0 %shard_map.76 = f32[768,2048]{1,0:T(8,128)S(1)} custom-call(bf16[768,1024]{1,0:T(8,128)(2,1)S(1)} %slice.194.left_ref, bf16[1024,2048]{1,0:T(8,128)(2,1)S(1)} %pad_maximum_fusion.right_ref), custom_call_target="tpu_custom_call" | custom-call | flops 3221225472 | bytes 12058624 | tf_op jit(solution)/shard_map/pallas_call | solution.py:87
  50.9 2.4 collective-permute-start.18
  54.6 4.2 %collective-permute-done.18 = bf16[256,512]{1,0:T(8,128)(2,1)S(1)} collective-permute-done((bf16[256,512]{1,0:T(8,128)(2,1)S(1)}, bf16[256,512]{1,0:T(8,128)(2,1)S(1)}, u32[]{:S(2)}, u32[]{:S(2)}) %collective-permute-start.18) | collective-permute-done | bytes 262176 | tf_op jit(solution)/shard_map/ppermute | solution.py:43
  60.7 1.5 collective-permute-start.10
  62.7 1.3 copy-done.17
  64.0 2.1 pad_maximum_fusion.1.right_ref
  66.5 3.0 %collective-permute-start.14 = (bf16[128,2048]{1,0:T(8,128)(2,1)}, bf16[128,2048]{1,0:T(8,128)(2,1)}, u32[]{:S(2)}, u32[]{:S(2)}) collective-permute-start(bf16[128,2048]{1,0:T(8,128)(2,1)} %get-tuple-element.64), channel_id=1, source_target_pairs={{0,12},{1,13},{2,14},{3,15},{4,0},{5,1},{6,2},{7,3},{8,4},{9,5},{1... | collective-permute-start | bytes 1572872 | tf_op jit(solution)/shard_map/ppermute | solution.py:43
  69.8 8.2 %shard_map.77 = f32[1024,2048]{1,0:T(8,128)S(1)} custom-call(bf16[1024,1024]{1,0:T(8,128)(2,1)S(1)} %pad_maximum_fusion.8.left_ref.right_ref, bf16[2048,1024]{1,0:T(8,128)(2,1)S(1)} %pad_maximum_fusion.1.right_ref), custom_call_target="tpu_custom_call" | custom-call | flops 4294967296 | bytes 14680064 | tf_op jit(solution)/shard_map/pallas_call | solution.py:87
  78.0 1.3 copy-done.11
  80.3 3.2 %collective-permute-start.29 = (bf16[128,2048]{1,0:T(8,128)(2,1)S(1)}, bf16[128,2048]{1,0:T(8,128)(2,1)S(1)}, u32[]{:S(2)}, u32[]{:S(2)}) collective-permute-start(bf16[128,2048]{1,0:T(8,128)(2,1)S(1)} %get-tuple-element.66), channel_id=1, source_target_pairs={{0,12},{1,13},{2,14},{3,15},{4,0},{5,1},{6,2},{7,3},{8,4},{9,5},{1... | collective-permute-start | bytes 1572872 | tf_op jit(solution)/shard_map/ppermute | solution.py:43
  83.5 6.2 %collective-permute-done.12 = bf16[128,2048]{1,0:T(8,128)(2,1)} collective-permute-done((bf16[128,2048]{1,0:T(8,128)(2,1)}, bf16[128,2048]{1,0:T(8,128)(2,1)}, u32[]{:S(2)}, u32[]{:S(2)}) %collective-permute-start.12) | collective-permute-done | bytes 524320 | tf_op jit(solution)/shard_map/ppermute | solution.py:43
  89.8 1.7 fusion.13
  92.7 3.2 %collective-permute-start.26 = (bf16[128,2048]{1,0:T(8,128)(2,1)S(1)}, bf16[128,2048]{1,0:T(8,128)(2,1)S(1)}, u32[]{:S(2)}, u32[]{:S(2)}) collective-permute-start(bf16[128,2048]{1,0:T(8,128)(2,1)S(1)} %get-tuple-element.67), channel_id=1, source_target_pairs={{0,12},{1,13},{2,14},{3,15},{4,0},{5,1},{6,2},{7,3},{8,4},{9,5},{1... | collective-permute-start | bytes 1572872 | tf_op jit(solution)/shard_map/ppermute | solution.py:43
  96.0 4.9 %collective-permute-done.27 = bf16[128,2048]{1,0:T(8,128)(2,1)S(1)} collective-permute-done((bf16[128,2048]{1,0:T(8,128)(2,1)S(1)}, bf16[128,2048]{1,0:T(8,128)(2,1)S(1)}, u32[]{:S(2)}, u32[]{:S(2)}) %collective-permute-start.27) | collective-permute-done | bytes 524320 | tf_op jit(solution)/shard_map/ppermute | solution.py:43
  101.3 3.2 %collective-permute-start.30 = (bf16[128,2048]{1,0:T(8,128)(2,1)S(1)}, bf16[128,2048]{1,0:T(8,128)(2,1)S(1)}, u32[]{:S(2)}, u32[]{:S(2)}) collective-permute-start(bf16[128,2048]{1,0:T(8,128)(2,1)S(1)} %get-tuple-element.56), channel_id=1, source_target_pairs={{0,12},{1,13},{2,14},{3,15},{4,0},{5,1},{6,2},{7,3},{8,4},{9,5},{1... | collective-permute-start | bytes 1572872 | tf_op jit(solution)/shard_map/ppermute | solution.py:43
  104.5 10.8 %collective-permute-done.21 = bf16[256,2048]{1,0:T(8,128)(2,1)S(1)} collective-permute-done((bf16[256,2048]{1,0:T(8,128)(2,1)S(1)}, bf16[256,2048]{1,0:T(8,128)(2,1)S(1)}, u32[]{:S(2)}, u32[]{:S(2)}) %collective-permute-start.21) | collective-permute-done | bytes 1048608 | tf_op jit(solution)/shard_map/ppermute | solution.py:43
  115.4 2.3 fusion.3
  117.7 5.0 %collective-permute-done.28 = bf16[128,2048]{1,0:T(8,128)(2,1)S(1)} collective-permute-done((bf16[128,2048]{1,0:T(8,128)(2,1)S(1)}, bf16[128,2048]{1,0:T(8,128)(2,1)S(1)}, u32[]{:S(2)}, u32[]{:S(2)}) %collective-permute-start.28) | collective-permute-done | bytes 524320 | tf_op jit(solution)/shard_map/ppermute | solution.py:43
  126.6 1.8 collective-permute-start.22
  128.4 21.7 %collective-permute-done.31 = bf16[256,2048]{1,0:T(8,128)(2,1)} collective-permute-done((bf16[256,2048]{1,0:T(8,128)(2,1)}, bf16[256,2048]{1,0:T(8,128)(2,1)}, u32[]{:S(2)}, u32[]{:S(2)}) %collective-permute-start.31) | collective-permute-done | bytes 1048608 | tf_op jit(solution)/shard_map/ppermute | solution.py:43
  150.1 2.7 multiply_convert_fusion
  153.4 1.5 collective-permute-start.39
  157.1 3.3 %collective-permute-start.32 = (bf16[128,2048]{1,0:T(8,128)(2,1)S(1)}, bf16[128,2048]{1,0:T(8,128)(2,1)S(1)}, u32[]{:S(2)}, u32[]{:S(2)}) collective-permute-start(bf16[128,2048]{1,0:T(8,128)(2,1)S(1)} %slice.214), channel_id=1, source_target_pairs={{0,12},{1,13},{2,14},{3,15},{4,0},{5,1},{6,2},{7,3},{8,4},{9,5},{1... | collective-permute-start | bytes 1572872 | tf_op jit(solution)/shard_map/ppermute | solution.py:43
  160.4 2.0 pad_maximum_fusion.5.left_ref
  162.4 6.2 %shard_map.78 = f32[768,1024]{1,0:T(8,128)S(1)} custom-call(bf16[768,2048]{1,0:T(8,128)(2,1)S(1)} %pad_maximum_fusion.5.left_ref, bf16[2048,1024]{1,0:T(8,128)(2,1)S(1)} %copy-done.3), custom_call_target="tpu_custom_call" | custom-call | flops 3221225472 | bytes 10485760 | tf_op jit(solution)/shard_map/pallas_call | solution.py:87
  168.9 20.5 %collective-permute-done.23 = bf16[128,2048]{1,0:T(8,128)(2,1)S(1)} collective-permute-done((bf16[128,2048]{1,0:T(8,128)(2,1)S(1)}, bf16[128,2048]{1,0:T(8,128)(2,1)S(1)}, u32[]{:S(2)}, u32[]{:S(2)}) %collective-permute-start.23) | collective-permute-done | bytes 524320 | tf_op jit(solution)/shard_map/ppermute | solution.py:43
  189.5 1.8 shard_map.79
  191.7 2.3 pad_maximum_fusion.2.left_ref
  194.0 6.3 %shard_map.80 = bf16[2048,1024]{1,0:T(8,128)(2,1)S(1)} custom-call(bf16[1024,2048]{1,0:T(8,128)(2,1)S(1)} %pad_maximum_fusion.2.left_ref, bf16[1024,1024]{1,0:T(8,128)(2,1)S(1)} %copy-done.12), custom_call_target="tpu_custom_call" | custom-call | flops 4294967296 | bytes 10485760 | tf_op jit(solution)/shard_map/pallas_call | solution.py:87
  200.4 1.7 slice.217
  203.5 1.7 copy-done.1
  205.2 5.9 %shard_map.81 = f32[768,1024]{1,0:T(8,128)S(1)} custom-call(bf16[768,2048]{1,0:T(8,128)(2,1)S(1)} %pad_maximum_fusion.6.left_ref.refs_2_, bf16[1024,2048]{1,0:T(8,128)(2,1)S(1)} %copy-done.1), custom_call_target="tpu_custom_call" | custom-call | flops 3221225472 | bytes 10485760 | tf_op jit(solution)/shard_map/pallas_call | solution.py:87
  211.2 1.5 slice.222
  215.4 3.0 %collective-permute-start.42 = (bf16[128,2048]{1,0:T(8,128)(2,1)S(1)}, bf16[128,2048]{1,0:T(8,128)(2,1)S(1)}, u32[]{:S(2)}, u32[]{:S(2)}) collective-permute-start(bf16[128,2048]{1,0:T(8,128)(2,1)S(1)} %slice.185), channel_id=1, source_target_pairs={{0,12},{1,13},{2,14},{3,15},{4,0},{5,1},{6,2},{7,3},{8,4},{9,5},{1... | collective-permute-start | bytes 1572872 | tf_op jit(solution)/shard_map/ppermute | solution.py:43
  218.4 10.3 %collective-permute-done.40 = bf16[128,2048]{1,0:T(8,128)(2,1)S(1)} collective-permute-done((bf16[128,2048]{1,0:T(8,128)(2,1)S(1)}, bf16[128,2048]{1,0:T(8,128)(2,1)S(1)}, u32[]{:S(2)}, u32[]{:S(2)}) %collective-permute-start.40) | collective-permute-done | bytes 524320 | tf_op jit(solution)/shard_map/ppermute | solution.py:43
  228.7 1.5 collective-permute-done.42
  230.3 1.6 shard_map.82
  233.3 2.2 slice_add_fusion
  237.1 1.5 copy-done.7
  238.9 6.0 %shard_map.83 = bf16[1024,2048]{1,0:T(8,128)(2,1)S(1)} custom-call(bf16[1024,1024]{1,0:T(8,128)(2,1)S(1)} %pad_maximum_fusion.7.refs_0_, bf16[256,2048]{1,0:T(8,128)(2,1)S(1)} %copy-done.10, bf16[768,2048]{1,0:T(8,128)(2,1)S(1)} %copy-done.7), custom_call_target="tpu_custom_call" | custom-call | flops 4294967296 | bytes 6291456 | tf_op jit(solution)/shard_map/pallas_call | solution.py:114
  247.5 2.6 collective-permute-start.37
  250.1 10.8 %collective-permute-done.35 = bf16[256,512]{1,0:T(8,128)(2,1)S(1)} collective-permute-done((bf16[256,512]{1,0:T(8,128)(2,1)S(1)}, bf16[256,512]{1,0:T(8,128)(2,1)S(1)}, u32[]{:S(2)}, u32[]{:S(2)}) %collective-permute-start.35) | collective-permute-done | bytes 262176 | tf_op jit(solution)/shard_map/ppermute | solution.py:43
  260.9 1.7 collective-permute-start.46
  262.6 1.6 collective-permute-start.47
  264.2 1.4 convert_add_fusion.2
  265.6 9.1 %collective-permute-done.45 = bf16[256,512]{1,0:T(8,128)(2,1)S(1)} collective-permute-done((bf16[256,512]{1,0:T(8,128)(2,1)S(1)}, bf16[256,512]{1,0:T(8,128)(2,1)S(1)}, u32[]{:S(2)}, u32[]{:S(2)}) %collective-permute-start.45) | collective-permute-done | bytes 262176 | tf_op jit(solution)/shard_map/ppermute | solution.py:43
  274.7 2.6 collective-permute-start.38
  278.5 6.9 %collective-permute-done.38 = f32[128,512]{1,0:T(8,128)S(1)} collective-permute-done((f32[128,512]{1,0:T(8,128)S(1)}, f32[128,512]{1,0:T(8,128)S(1)}, u32[]{:S(2)}, u32[]{:S(2)}) %collective-permute-start.38) | collective-permute-done | bytes 262176 | tf_op jit(solution)/shard_map/ppermute | solution.py:43
  286.1 2.8 collective-permute-done.48
  290.4 2.3 pad_maximum_fusion.4
  292.7 2.5 pad_maximum_fusion.3
  (167 shorter events, 34.7 us)
Async XLA Ops:
  0.6 13.4 %collective-permute-start = (bf16[128,512]{1,0:T(8,128)(2,1)}, bf16[128,512]{1,0:T(8,128)(2,1)S(1)}, u32[]{:S(2)}, u32[]{:S(2)}) collective-permute-start(bf16[128,512]{1,0:T(8,128)(2,1)} %param.4), channel_id=1, source_target_pairs={{0,16},{1,17},{2,18},{3,19},{4,20},{5,21},{6,22},{7,23},{8,24},{9,... | collective-permute-start | bytes 393224 | tf_op jit(solution)/shard_map/ppermute | solution.py:43
  4.0 12.0 %collective-permute-start.1 = (bf16[128,512]{1,0:T(8,128)(2,1)}, bf16[128,512]{1,0:T(8,128)(2,1)S(1)}, u32[]{:S(2)}, u32[]{:S(2)}) collective-permute-start(bf16[128,512]{1,0:T(8,128)(2,1)} %param.4), channel_id=1, source_target_pairs={{0,96},{1,97},{2,98},{3,99},{4,100},{5,101},{6,102},{7,103},{8,104... | collective-permute-start | bytes 393224 | tf_op jit(solution)/shard_map/ppermute | solution.py:43
  8.1 17.0 %collective-permute-start.3 = (bf16[128,512]{1,0:T(8,128)(2,1)}, bf16[128,512]{1,0:T(8,128)(2,1)S(1)}, u32[]{:S(2)}, u32[]{:S(2)}) collective-permute-start(bf16[128,512]{1,0:T(8,128)(2,1)} %param.4), channel_id=1, source_target_pairs={{0,64},{1,65},{2,66},{3,67},{4,68},{5,69},{6,70},{7,71},{8,72},{9,... | collective-permute-start | bytes 393224 | tf_op jit(solution)/shard_map/ppermute | solution.py:43
  8.1 17.0 %collective-permute-start.5 = (bf16[128,512]{1,0:T(8,128)(2,1)}, bf16[128,512]{1,0:T(8,128)(2,1)S(1)}, u32[]{:S(2)}, u32[]{:S(2)}) collective-permute-start(bf16[128,512]{1,0:T(8,128)(2,1)} %param.4), channel_id=1, source_target_pairs={{0,32},{1,33},{2,34},{3,35},{4,36},{5,37},{6,38},{7,39},{8,40},{9,... | collective-permute-start | bytes 393224 | tf_op jit(solution)/shard_map/ppermute | solution.py:43
  9.3 4.5 %copy-start.20 = (bf16[128,512]{1,0:T(8,128)(2,1)S(1)}, bf16[128,512]{1,0:T(8,128)(2,1)}, u32[]{:S(2)}) copy-start(bf16[128,512]{1,0:T(8,128)(2,1)} %param.4) | copy-start | bytes 393220
  13.9 16.9 %collective-permute-start.8 = (bf16[512,2048]{1,0:T(8,128)(2,1)}, bf16[512,2048]{1,0:T(8,128)(2,1)}, u32[]{:S(2)}, u32[]{:S(2)}) collective-permute-start(bf16[512,2048]{1,0:T(8,128)(2,1)} %get-tuple-element.73), channel_id=1, source_target_pairs={{0,1},{1,0},{2,3},{3,2},{4,5},{5,4},{6,7},{7,6},{8,9},{9,8},{10,11... | collective-permute-start | bytes 6291464 | tf_op jit(solution)/shard_map/ppermute | solution.py:43
  14.0 6.6 %collective-permute-start.2 = (bf16[128,512]{1,0:T(8,128)(2,1)S(1)}, bf16[128,512]{1,0:T(8,128)(2,1)S(1)}, u32[]{:S(2)}, u32[]{:S(2)}) collective-permute-start(bf16[128,512]{1,0:T(8,128)(2,1)S(1)} %collective-permute-done), channel_id=1, source_target_pairs={{0,96},{1,97},{2,98},{3,99},{4,100},{5,101},{6,102},{7,103},{8,104... | collective-permute-start | bytes 393224 | tf_op jit(solution)/shard_map/ppermute | solution.py:43
  16.1 9.0 %collective-permute-start.4 = (bf16[128,512]{1,0:T(8,128)(2,1)S(1)}, bf16[128,512]{1,0:T(8,128)(2,1)S(1)}, u32[]{:S(2)}, u32[]{:S(2)}) collective-permute-start(bf16[128,512]{1,0:T(8,128)(2,1)S(1)} %collective-permute-done), channel_id=1, source_target_pairs={{0,64},{1,65},{2,66},{3,67},{4,68},{5,69},{6,70},{7,71},{8,72},{9,... | collective-permute-start | bytes 393224 | tf_op jit(solution)/shard_map/ppermute | solution.py:43
  20.6 6.9 %collective-permute-start.6 = (bf16[128,512]{1,0:T(8,128)(2,1)S(1)}, bf16[128,512]{1,0:T(8,128)(2,1)S(1)}, u32[]{:S(2)}, u32[]{:S(2)}) collective-permute-start(bf16[128,512]{1,0:T(8,128)(2,1)S(1)} %collective-permute-done), channel_id=1, source_target_pairs={{0,32},{1,33},{2,34},{3,35},{4,36},{5,37},{6,38},{7,39},{8,40},{9,... | collective-permute-start | bytes 393224 | tf_op jit(solution)/shard_map/ppermute | solution.py:43
  27.6 2.3 copy-start.16
  27.7 2.7 collective-permute-start.7
  28.4 11.3 %collective-permute-start.15 = (bf16[128,512]{1,0:T(8,128)(2,1)S(1)}, bf16[128,512]{1,0:T(8,128)(2,1)S(1)}, u32[]{:S(2)}, u32[]{:S(2)}) collective-permute-start(bf16[128,512]{1,0:T(8,128)(2,1)S(1)} %copy-done.21), channel_id=1, source_target_pairs={{0,16},{1,17},{2,18},{3,19},{4,20},{5,21},{6,22},{7,23},{8,24},{9,... | collective-permute-start | bytes 393224 | tf_op jit(solution)/shard_map/ppermute | solution.py:43
  30.1 32.6 %collective-permute-start.20 = (bf16[2048,512]{1,0:T(8,128)(2,1)S(1)}, bf16[2048,512]{1,0:T(8,128)(2,1)S(1)}, u32[]{:S(2)}, u32[]{:S(2)}) collective-permute-start(bf16[2048,512]{1,0:T(8,128)(2,1)S(1)} %get-tuple-element.71), channel_id=1, source_target_pairs={{0,1},{1,0},{2,3},{3,2},{4,5},{5,4},{6,7},{7,6},{8,9},{9,8},{10,11... | collective-permute-start | bytes 6291464 | tf_op jit(solution)/shard_map/ppermute | solution.py:43
  33.8 10.6 %copy-start = (bf16[1024,2048]{1,0:T(8,128)(2,1)}, bf16[1024,2048]{1,0:T(8,128)(2,1)S(1)}, u32[]{:S(2)}) copy-start(bf16[1024,2048]{1,0:T(8,128)(2,1)S(1)} %pad_maximum_fusion.right_ref) | copy-start | bytes 12582916
  36.4 14.5 %collective-permute-start.11 = (bf16[128,2048]{1,0:T(8,128)(2,1)S(1)}, bf16[128,2048]{1,0:T(8,128)(2,1)S(1)}, u32[]{:S(2)}, u32[]{:S(2)}) collective-permute-start(bf16[128,2048]{1,0:T(8,128)(2,1)S(1)} %get-tuple-element.91), channel_id=1, source_target_pairs={{0,4},{1,5},{2,6},{3,7},{4,8},{5,9},{6,10},{7,11},{8,12},{9,13},{1... | collective-permute-start | bytes 1572872 | tf_op jit(solution)/shard_map/ppermute | solution.py:43
  38.0 15.3 %collective-permute-start.13 = (bf16[128,2048]{1,0:T(8,128)(2,1)S(1)}, bf16[128,2048]{1,0:T(8,128)(2,1)S(1)}, u32[]{:S(2)}, u32[]{:S(2)}) collective-permute-start(bf16[128,2048]{1,0:T(8,128)(2,1)S(1)} %get-tuple-element.90), channel_id=1, source_target_pairs={{0,12},{1,13},{2,14},{3,15},{4,0},{5,1},{6,2},{7,3},{8,4},{9,5},{1... | collective-permute-start | bytes 1572872 | tf_op jit(solution)/shard_map/ppermute | solution.py:43
  39.8 14.8 %collective-permute-start.16 = (bf16[256,512]{1,0:T(8,128)(2,1)S(1)}, bf16[256,512]{1,0:T(8,128)(2,1)S(1)}, u32[]{:S(2)}, u32[]{:S(2)}) collective-permute-start(bf16[256,512]{1,0:T(8,128)(2,1)S(1)} %constant_dynamic-update-slice_fusion.8), channel_id=1, source_target_pairs={{0,96},{1,97},{2,98},{3,99},{4,100},{5,101},{6,102},{7,103},{8,104... | collective-permute-start | bytes 786440 | tf_op jit(solution)/shard_map/ppermute | solution.py:43
  40.6 14.0 %collective-permute-start.17 = (bf16[256,512]{1,0:T(8,128)(2,1)S(1)}, bf16[256,512]{1,0:T(8,128)(2,1)S(1)}, u32[]{:S(2)}, u32[]{:S(2)}) collective-permute-start(bf16[256,512]{1,0:T(8,128)(2,1)S(1)} %constant_dynamic-update-slice_fusion.8), channel_id=1, source_target_pairs={{0,64},{1,65},{2,66},{3,67},{4,68},{5,69},{6,70},{7,71},{8,72},{9,... | collective-permute-start | bytes 786440 | tf_op jit(solution)/shard_map/ppermute | solution.py:43
  50.9 7.9 %collective-permute-start.18 = (bf16[256,512]{1,0:T(8,128)(2,1)S(1)}, bf16[256,512]{1,0:T(8,128)(2,1)S(1)}, u32[]{:S(2)}, u32[]{:S(2)}) collective-permute-start(bf16[256,512]{1,0:T(8,128)(2,1)S(1)} %constant_dynamic-update-slice_fusion.8), channel_id=1, source_target_pairs={{0,32},{1,33},{2,34},{3,35},{4,36},{5,37},{6,38},{7,39},{8,40},{9,... | collective-permute-start | bytes 786440 | tf_op jit(solution)/shard_map/ppermute | solution.py:43
  59.1 10.4 %collective-permute-start.19 = (bf16[1024,512]{1,0:T(8,128)(2,1)S(1)}, bf16[1024,512]{1,0:T(8,128)(2,1)S(1)}, u32[]{:S(2)}, u32[]{:S(2)}) collective-permute-start(bf16[1024,512]{1,0:T(8,128)(2,1)S(1)} %pad_maximum_fusion.14), channel_id=1, source_target_pairs={{0,1},{1,0},{2,3},{3,2},{4,5},{5,4},{6,7},{7,6},{8,9},{9,8},{10,11... | collective-permute-start | bytes 3145736 | tf_op jit(solution)/shard_map/ppermute | solution.py:43
  60.7 19.6 %collective-permute-start.10 = (bf16[128,2048]{1,0:T(8,128)(2,1)}, bf16[128,2048]{1,0:T(8,128)(2,1)S(1)}, u32[]{:S(2)}, u32[]{:S(2)}) collective-permute-start(bf16[128,2048]{1,0:T(8,128)(2,1)} %get-tuple-element.76), channel_id=1, source_target_pairs={{0,12},{1,13},{2,14},{3,15},{4,0},{5,1},{6,2},{7,3},{8,4},{9,5},{1... | collective-permute-start | bytes 1572872 | tf_op jit(solution)/shard_map/ppermute | solution.py:43
  62.2 21.3 %collective-permute-start.9 = (bf16[128,2048]{1,0:T(8,128)(2,1)}, bf16[128,2048]{1,0:T(8,128)(2,1)S(1)}, u32[]{:S(2)}, u32[]{:S(2)}) collective-permute-start(bf16[128,2048]{1,0:T(8,128)(2,1)} %get-tuple-element.77), channel_id=1, source_target_pairs={{0,4},{1,5},{2,6},{3,7},{4,8},{5,9},{6,10},{7,11},{8,12},{9,13},{1... | collective-permute-start | bytes 1572872 | tf_op jit(solution)/shard_map/ppermute | solution.py:43
  66.1 3.6 %copy-start.2 = (bf16[2048,1024]{1,0:T(8,128)(2,1)}, bf16[2048,1024]{1,0:T(8,128)(2,1)S(1)}, u32[]{:S(2)}) copy-start(bf16[2048,1024]{1,0:T(8,128)(2,1)S(1)} %pad_maximum_fusion.1.right_ref) | copy-start | bytes 12582916
  66.1 23.6 %collective-permute-start.12 = (bf16[128,2048]{1,0:T(8,128)(2,1)}, bf16[128,2048]{1,0:T(8,128)(2,1)}, u32[]{:S(2)}, u32[]{:S(2)}) collective-permute-start(bf16[128,2048]{1,0:T(8,128)(2,1)} %get-tuple-element.65), channel_id=1, source_target_pairs={{0,4},{1,5},{2,6},{3,7},{4,8},{5,9},{6,10},{7,11},{8,12},{9,13},{1... | collective-permute-start | bytes 1572872 | tf_op jit(solution)/shard_map/ppermute | solution.py:43
  66.5 23.3 %collective-permute-start.14 = (bf16[128,2048]{1,0:T(8,128)(2,1)}, bf16[128,2048]{1,0:T(8,128)(2,1)}, u32[]{:S(2)}, u32[]{:S(2)}) collective-permute-start(bf16[128,2048]{1,0:T(8,128)(2,1)} %get-tuple-element.64), channel_id=1, source_target_pairs={{0,12},{1,13},{2,14},{3,15},{4,0},{5,1},{6,2},{7,3},{8,4},{9,5},{1... | collective-permute-start | bytes 1572872 | tf_op jit(solution)/shard_map/ppermute | solution.py:43
  80.2 20.7 %collective-permute-start.27 = (bf16[128,2048]{1,0:T(8,128)(2,1)S(1)}, bf16[128,2048]{1,0:T(8,128)(2,1)S(1)}, u32[]{:S(2)}, u32[]{:S(2)}) collective-permute-start(bf16[128,2048]{1,0:T(8,128)(2,1)S(1)} %get-tuple-element.69), channel_id=1, source_target_pairs={{0,4},{1,5},{2,6},{3,7},{4,8},{5,9},{6,10},{7,11},{8,12},{9,13},{1... | collective-permute-start | bytes 1572872 | tf_op jit(solution)/shard_map/ppermute | solution.py:43
  80.3 20.6 %collective-permute-start.29 = (bf16[128,2048]{1,0:T(8,128)(2,1)S(1)}, bf16[128,2048]{1,0:T(8,128)(2,1)S(1)}, u32[]{:S(2)}, u32[]{:S(2)}) collective-permute-start(bf16[128,2048]{1,0:T(8,128)(2,1)S(1)} %get-tuple-element.66), channel_id=1, source_target_pairs={{0,12},{1,13},{2,14},{3,15},{4,0},{5,1},{6,2},{7,3},{8,4},{9,5},{1... | collective-permute-start | bytes 1572872 | tf_op jit(solution)/shard_map/ppermute | solution.py:43
  91.6 23.8 %collective-permute-start.21 = (bf16[256,2048]{1,0:T(8,128)(2,1)S(1)}, bf16[256,2048]{1,0:T(8,128)(2,1)S(1)}, u32[]{:S(2)}, u32[]{:S(2)}) collective-permute-start(bf16[256,2048]{1,0:T(8,128)(2,1)S(1)} %fusion.5), channel_id=1, source_target_pairs={{0,2},{1,3},{2,0},{3,1},{4,6},{5,7},{6,4},{7,5},{8,10},{9,11},{10,... | collective-permute-start | bytes 3145736 | tf_op jit(solution)/shard_map/ppermute | solution.py:43
  92.7 24.9 %collective-permute-start.25 = (bf16[128,2048]{1,0:T(8,128)(2,1)S(1)}, bf16[128,2048]{1,0:T(8,128)(2,1)S(1)}, u32[]{:S(2)}, u32[]{:S(2)}) collective-permute-start(bf16[128,2048]{1,0:T(8,128)(2,1)S(1)} %get-tuple-element.68), channel_id=1, source_target_pairs={{0,4},{1,5},{2,6},{3,7},{4,8},{5,9},{6,10},{7,11},{8,12},{9,13},{1... | collective-permute-start | bytes 1572872 | tf_op jit(solution)/shard_map/ppermute | solution.py:43
  92.7 24.9 %collective-permute-start.26 = (bf16[128,2048]{1,0:T(8,128)(2,1)S(1)}, bf16[128,2048]{1,0:T(8,128)(2,1)S(1)}, u32[]{:S(2)}, u32[]{:S(2)}) collective-permute-start(bf16[128,2048]{1,0:T(8,128)(2,1)S(1)} %get-tuple-element.67), channel_id=1, source_target_pairs={{0,12},{1,13},{2,14},{3,15},{4,0},{5,1},{6,2},{7,3},{8,4},{9,5},{1... | collective-permute-start | bytes 1572872 | tf_op jit(solution)/shard_map/ppermute | solution.py:43
  101.2 21.4 %collective-permute-start.28 = (bf16[128,2048]{1,0:T(8,128)(2,1)S(1)}, bf16[128,2048]{1,0:T(8,128)(2,1)S(1)}, u32[]{:S(2)}, u32[]{:S(2)}) collective-permute-start(bf16[128,2048]{1,0:T(8,128)(2,1)S(1)} %get-tuple-element.57), channel_id=1, source_target_pairs={{0,4},{1,5},{2,6},{3,7},{4,8},{5,9},{6,10},{7,11},{8,12},{9,13},{1... | collective-permute-start | bytes 1572872 | tf_op jit(solution)/shard_map/ppermute | solution.py:43
  101.3 21.3 %collective-permute-start.30 = (bf16[128,2048]{1,0:T(8,128)(2,1)S(1)}, bf16[128,2048]{1,0:T(8,128)(2,1)S(1)}, u32[]{:S(2)}, u32[]{:S(2)}) collective-permute-start(bf16[128,2048]{1,0:T(8,128)(2,1)S(1)} %get-tuple-element.56), channel_id=1, source_target_pairs={{0,12},{1,13},{2,14},{3,15},{4,0},{5,1},{6,2},{7,3},{8,4},{9,5},{1... | collective-permute-start | bytes 1572872 | tf_op jit(solution)/shard_map/ppermute | solution.py:43
  125.3 24.7 %collective-permute-start.31 = (bf16[256,2048]{1,0:T(8,128)(2,1)}, bf16[256,2048]{1,0:T(8,128)(2,1)}, u32[]{:S(2)}, u32[]{:S(2)}) collective-permute-start(bf16[256,2048]{1,0:T(8,128)(2,1)} %fusion.4), channel_id=1, source_target_pairs={{0,2},{1,3},{2,0},{3,1},{4,6},{5,7},{6,4},{7,5},{8,10},{9,11},{10,... | collective-permute-start | bytes 3145736 | tf_op jit(solution)/shard_map/ppermute | solution.py:43
  126.3 28.5 %collective-permute-start.24 = (bf16[256,2048]{1,0:T(8,128)(2,1)}, bf16[256,2048]{1,0:T(8,128)(2,1)}, u32[]{:S(2)}, u32[]{:S(2)}) collective-permute-start(bf16[256,2048]{1,0:T(8,128)(2,1)} %get-tuple-element.38), channel_id=1, source_target_pairs={{0,12},{1,13},{2,14},{3,15},{4,0},{5,1},{6,2},{7,3},{8,4},{9,5},{1... | collective-permute-start | bytes 3145736 | tf_op jit(solution)/shard_map/ppermute | solution.py:43
  126.6 28.2 %collective-permute-start.22 = (bf16[256,2048]{1,0:T(8,128)(2,1)}, bf16[256,2048]{1,0:T(8,128)(2,1)}, u32[]{:S(2)}, u32[]{:S(2)}) collective-permute-start(bf16[256,2048]{1,0:T(8,128)(2,1)} %get-tuple-element.38), channel_id=1, source_target_pairs={{0,4},{1,5},{2,6},{3,7},{4,8},{5,9},{6,10},{7,11},{8,12},{9,13},{1... | collective-permute-start | bytes 3145736 | tf_op jit(solution)/shard_map/ppermute | solution.py:43
  152.8 50.3 %collective-permute-start.41 = (bf16[256,2048]{1,0:T(8,128)(2,1)S(1)}, bf16[256,2048]{1,0:T(8,128)(2,1)S(1)}, u32[]{:S(2)}, u32[]{:S(2)}) collective-permute-start(bf16[256,2048]{1,0:T(8,128)(2,1)S(1)} %multiply_convert_fusion), channel_id=1, source_target_pairs={{0,12},{1,13},{2,14},{3,15},{4,0},{5,1},{6,2},{7,3},{8,4},{9,5},{1... | collective-permute-start | bytes 3145736 | tf_op jit(solution)/shard_map/ppermute | solution.py:43
  153.4 49.6 %collective-permute-start.39 = (bf16[256,2048]{1,0:T(8,128)(2,1)S(1)}, bf16[256,2048]{1,0:T(8,128)(2,1)S(1)}, u32[]{:S(2)}, u32[]{:S(2)}) collective-permute-start(bf16[256,2048]{1,0:T(8,128)(2,1)S(1)} %multiply_convert_fusion), channel_id=1, source_target_pairs={{0,4},{1,5},{2,6},{3,7},{4,8},{5,9},{6,10},{7,11},{8,12},{9,13},{1... | collective-permute-start | bytes 3145736 | tf_op jit(solution)/shard_map/ppermute | solution.py:43
  155.9 33.5 %collective-permute-start.23 = (bf16[128,2048]{1,0:T(8,128)(2,1)S(1)}, bf16[128,2048]{1,0:T(8,128)(2,1)S(1)}, u32[]{:S(2)}, u32[]{:S(2)}) collective-permute-start(bf16[128,2048]{1,0:T(8,128)(2,1)S(1)} %slice.207), channel_id=1, source_target_pairs={{0,4},{1,5},{2,6},{3,7},{4,8},{5,9},{6,10},{7,11},{8,12},{9,13},{1... | collective-permute-start | bytes 1572872 | tf_op jit(solution)/shard_map/ppermute | solution.py:43
  157.1 5.3 %copy-start.3 = (bf16[2048,1024]{1,0:T(8,128)(2,1)S(1)}, bf16[2048,1024]{1,0:T(8,128)(2,1)}, u32[]{:S(2)}) copy-start(bf16[2048,1024]{1,0:T(8,128)(2,1)} %copy-done.2) | copy-start | bytes 12582916
  157.1 32.3 %collective-permute-start.32 = (bf16[128,2048]{1,0:T(8,128)(2,1)S(1)}, bf16[128,2048]{1,0:T(8,128)(2,1)S(1)}, u32[]{:S(2)}, u32[]{:S(2)}) collective-permute-start(bf16[128,2048]{1,0:T(8,128)(2,1)S(1)} %slice.214), channel_id=1, source_target_pairs={{0,12},{1,13},{2,14},{3,15},{4,0},{5,1},{6,2},{7,3},{8,4},{9,5},{1... | collective-permute-start | bytes 1572872 | tf_op jit(solution)/shard_map/ppermute | solution.py:43
  168.8 45.0 %collective-permute-start.34 = (f32[768,512]{1,0:T(8,128)S(1)}, f32[768,512]{1,0:T(8,128)S(1)}, u32[]{:S(2)}, u32[]{:S(2)}) collective-permute-start(f32[768,512]{1,0:T(8,128)S(1)} %slice.213), channel_id=1, source_target_pairs={{0,1},{1,0},{2,3},{3,2},{4,5},{5,4},{6,7},{7,6},{8,9},{9,8},{10,11... | collective-permute-start | bytes 4718600 | tf_op jit(solution)/shard_map/ppermute | solution.py:43
  191.4 2.6 copy-start.12
  191.4 22.3 %collective-permute-start.33 = (f32[256,512]{1,0:T(8,128)S(1)}, f32[256,512]{1,0:T(8,128)S(1)}, u32[]{:S(2)}, u32[]{:S(2)}) collective-permute-start(f32[256,512]{1,0:T(8,128)S(1)} %get-tuple-element.84), channel_id=1, source_target_pairs={{0,1},{1,0},{2,3},{3,2},{4,5},{5,4},{6,7},{7,6},{8,9},{9,8},{10,11... | collective-permute-start | bytes 1572872 | tf_op jit(solution)/shard_map/ppermute | solution.py:43
  200.4 2.6 copy-start.4
  203.0 2.2 copy-start.1
  205.2 5.9 %copy-start.6 = (bf16[768,2048]{1,0:T(8,128)(2,1)}, bf16[768,2048]{1,0:T(8,128)(2,1)S(1)}, u32[]{:S(2)}) copy-start(bf16[768,2048]{1,0:T(8,128)(2,1)S(1)} %pad_maximum_fusion.6.left_ref.refs_2_) | copy-start | bytes 9437188
  211.2 2.2 copy-start.8
  213.3 15.4 %collective-permute-start.40 = (bf16[128,2048]{1,0:T(8,128)(2,1)S(1)}, bf16[128,2048]{1,0:T(8,128)(2,1)S(1)}, u32[]{:S(2)}, u32[]{:S(2)}) collective-permute-start(bf16[128,2048]{1,0:T(8,128)(2,1)S(1)} %slice.221), channel_id=1, source_target_pairs={{0,4},{1,5},{2,6},{3,7},{4,8},{5,9},{6,10},{7,11},{8,12},{9,13},{1... | collective-permute-start | bytes 1572872 | tf_op jit(solution)/shard_map/ppermute | solution.py:43
  213.3 20.0 %collective-permute-start.44 = (f32[768,512]{1,0:T(8,128)}, f32[768,512]{1,0:T(8,128)}, u32[]{:S(2)}, u32[]{:S(2)}) collective-permute-start(f32[768,512]{1,0:T(8,128)} %slice.222), channel_id=1, source_target_pairs={{0,1},{1,0},{2,3},{3,2},{4,5},{5,4},{6,7},{7,6},{8,9},{9,8},{10,11... | collective-permute-start | bytes 4718600 | tf_op jit(solution)/shard_map/ppermute | solution.py:43
  214.3 16.0 %copy-start.15 = (f32[1024,512]{1,0:T(8,128)}, f32[1024,512]{1,0:T(8,128)S(1)}, u32[]{:S(2)}) copy-start(f32[1024,512]{1,0:T(8,128)S(1)} %pad_maximum_fusion.11) | copy-start | bytes 6291460
  215.4 14.8 %collective-permute-start.42 = (bf16[128,2048]{1,0:T(8,128)(2,1)S(1)}, bf16[128,2048]{1,0:T(8,128)(2,1)S(1)}, u32[]{:S(2)}, u32[]{:S(2)}) collective-permute-start(bf16[128,2048]{1,0:T(8,128)(2,1)S(1)} %slice.185), channel_id=1, source_target_pairs={{0,12},{1,13},{2,14},{3,15},{4,0},{5,1},{6,2},{7,3},{8,4},{9,5},{1... | collective-permute-start | bytes 1572872 | tf_op jit(solution)/shard_map/ppermute | solution.py:43
  232.8 2.7 collective-permute-start.43
  232.8 56.8 %collective-permute-start.49 = (bf16[2048,512]{1,0:T(8,128)(2,1)}, bf16[2048,512]{1,0:T(8,128)(2,1)S(1)}, u32[]{:S(2)}, u32[]{:S(2)}) collective-permute-start(bf16[2048,512]{1,0:T(8,128)(2,1)} %slice.217), channel_id=1, source_target_pairs={{0,1},{1,0},{2,3},{3,2},{4,5},{5,4},{6,7},{7,6},{8,9},{9,8},{10,11... | collective-permute-start | bytes 6291464 | tf_op jit(solution)/shard_map/ppermute | solution.py:43
  244.9 2.2 copy-start.18
  245.1 44.5 %collective-permute-start.50 = (bf16[512,2048]{1,0:T(8,128)(2,1)S(1)}, bf16[512,2048]{1,0:T(8,128)(2,1)S(1)}, u32[]{:S(2)}, u32[]{:S(2)}) collective-permute-start(bf16[512,2048]{1,0:T(8,128)(2,1)S(1)} %slice.229), channel_id=1, source_target_pairs={{0,1},{1,0},{2,3},{3,2},{4,5},{5,4},{6,7},{7,6},{8,9},{9,8},{10,11... | collective-permute-start | bytes 6291464 | tf_op jit(solution)/shard_map/ppermute | solution.py:43
  245.9 15.0 %collective-permute-start.35 = (bf16[256,512]{1,0:T(8,128)(2,1)S(1)}, bf16[256,512]{1,0:T(8,128)(2,1)S(1)}, u32[]{:S(2)}, u32[]{:S(2)}) collective-permute-start(bf16[256,512]{1,0:T(8,128)(2,1)S(1)} %copy-done.19), channel_id=1, source_target_pairs={{0,32},{1,33},{2,34},{3,35},{4,36},{5,37},{6,38},{7,39},{8,40},{9,... | collective-permute-start | bytes 786440 | tf_op jit(solution)/shard_map/ppermute | solution.py:43
  247.1 13.8 %collective-permute-start.36 = (bf16[256,512]{1,0:T(8,128)(2,1)S(1)}, bf16[256,512]{1,0:T(8,128)(2,1)S(1)}, u32[]{:S(2)}, u32[]{:S(2)}) collective-permute-start(bf16[256,512]{1,0:T(8,128)(2,1)S(1)} %copy-done.18), channel_id=1, source_target_pairs={{0,64},{1,65},{2,66},{3,67},{4,68},{5,69},{6,70},{7,71},{8,72},{9,... | collective-permute-start | bytes 786440 | tf_op jit(solution)/shard_map/ppermute | solution.py:43
  247.5 15.0 %collective-permute-start.37 = (bf16[256,512]{1,0:T(8,128)(2,1)S(1)}, bf16[256,512]{1,0:T(8,128)(2,1)S(1)}, u32[]{:S(2)}, u32[]{:S(2)}) collective-permute-start(bf16[256,512]{1,0:T(8,128)(2,1)S(1)} %get-tuple-element.82), channel_id=1, source_target_pairs={{0,96},{1,97},{2,98},{3,99},{4,100},{5,101},{6,102},{7,103},{8,104... | collective-permute-start | bytes 786440 | tf_op jit(solution)/shard_map/ppermute | solution.py:43
  260.9 13.8 %collective-permute-start.45 = (bf16[256,512]{1,0:T(8,128)(2,1)S(1)}, bf16[256,512]{1,0:T(8,128)(2,1)S(1)}, u32[]{:S(2)}, u32[]{:S(2)}) collective-permute-start(bf16[256,512]{1,0:T(8,128)(2,1)S(1)} %get-tuple-element.78), channel_id=1, source_target_pairs={{0,32},{1,33},{2,34},{3,35},{4,36},{5,37},{6,38},{7,39},{8,40},{9,... | collective-permute-start | bytes 786440 | tf_op jit(solution)/shard_map/ppermute | solution.py:43
  260.9 16.4 %collective-permute-start.46 = (bf16[256,512]{1,0:T(8,128)(2,1)S(1)}, bf16[256,512]{1,0:T(8,128)(2,1)S(1)}, u32[]{:S(2)}, u32[]{:S(2)}) collective-permute-start(bf16[256,512]{1,0:T(8,128)(2,1)S(1)} %get-tuple-element.80), channel_id=1, source_target_pairs={{0,64},{1,65},{2,66},{3,67},{4,68},{5,69},{6,70},{7,71},{8,72},{9,... | collective-permute-start | bytes 786440 | tf_op jit(solution)/shard_map/ppermute | solution.py:43
  262.6 14.7 %collective-permute-start.47 = (bf16[256,512]{1,0:T(8,128)(2,1)S(1)}, bf16[256,512]{1,0:T(8,128)(2,1)S(1)}, u32[]{:S(2)}, u32[]{:S(2)}) collective-permute-start(bf16[256,512]{1,0:T(8,128)(2,1)S(1)} %get-tuple-element.79), channel_id=1, source_target_pairs={{0,96},{1,97},{2,98},{3,99},{4,100},{5,101},{6,102},{7,103},{8,104... | collective-permute-start | bytes 786440 | tf_op jit(solution)/shard_map/ppermute | solution.py:43
  264.2 25.4 %copy-start.5 = (bf16[2048,1024]{1,0:T(8,128)(2,1)S(1)}, bf16[2048,1024]{1,0:T(8,128)(2,1)}, u32[]{:S(2)}) copy-start(bf16[2048,1024]{1,0:T(8,128)(2,1)} %copy-done.4) | copy-start | bytes 12582916
  274.7 10.7 %collective-permute-start.38 = (f32[128,512]{1,0:T(8,128)S(1)}, f32[128,512]{1,0:T(8,128)S(1)}, u32[]{:S(2)}, u32[]{:S(2)}) collective-permute-start(f32[128,512]{1,0:T(8,128)S(1)} %slice.220), channel_id=1, source_target_pairs={{0,16},{1,17},{2,18},{3,19},{4,20},{5,21},{6,22},{7,23},{8,24},{9,... | collective-permute-start | bytes 786440 | tf_op jit(solution)/shard_map/ppermute | solution.py:43
  277.5 11.4 %collective-permute-start.48 = (f32[128,512]{1,0:T(8,128)S(1)}, f32[128,512]{1,0:T(8,128)S(1)}, u32[]{:S(2)}, u32[]{:S(2)}) collective-permute-start(f32[128,512]{1,0:T(8,128)S(1)} %slice.227), channel_id=1, source_target_pairs={{0,16},{1,17},{2,18},{3,19},{4,20},{5,21},{6,22},{7,23},{8,24},{9,... | collective-permute-start | bytes 786440 | tf_op jit(solution)/shard_map/ppermute | solution.py:43
  (9 other events, 12.7 us)
